TPU v7x, 128 devices: a whole 4x4x4 slice. The times are simulated.
128 devices in a mesh: slab: 4 (over z_hi, core), wide: 32 (over x, z_lo, y).
Axes of the slice: x: 4, y: 4, z: 4 (z_hi: 2, z_lo: 2; z = z_hi * 2 + z_lo), core: 2. Of those that a mesh axis runs over, the one named last changes fastest.
Arguments:
- orbitals: float32 [256, 128, 128, 128], P(None, 'slab', 'wide'), may hold values from -6 to 6
- points: int32 [512], replicated, may hold values from 0 to 2097151, as said below
Outputs:
- potential: float32 [128, 128, 128, 128], P(None, 'slab', 'wide')
Inputs may be any that keep to these rules, and one draw needn't show every extreme that they name: `points`: the 512 indices are distinct; how many fall in the cells of one device differs strongly between devices.
All inputs are finite; a program needn't handle non-finite values.
Results may differ from a plain program's by a relative error of at most 0.00014.
Values sent between devices are 32-bit elements; how exact they have to be, the bound alone decides.
No kernel may reach another device: no remote copies, remote signals or barrier semaphores. Data moves between devices by JAX's collectives and lax.ppermute only.
A program may use at most 192 MiB of HBM per device.

v0:
```python
import math

import jax
import jax.numpy as jnp
from jax import lax
from jax.sharding import PartitionSpec as P

VEC_DEV = 1


highest = lax.Precision.HIGHEST


def tables(length):
    index = jnp.arange(length, dtype=jnp.int32)
    phase = index[:, None] * index[None, :] % length
    angle = phase.astype(jnp.float32) * (2.0 * math.pi / length)
    return (jnp.cos(angle), jnp.sin(angle))


def contract(values, table, axis_pos):
    letters = "abcd"[: values.ndim]
    target = letters[:axis_pos] + "k" + letters[axis_pos + 1 :]
    return jnp.einsum(
        letters + "," + letters[axis_pos] + "k->" + target, values, table, precision=highest
    )


def rotate(stacked, axis_pos, sign, cosine, sine):
    real_part = stacked[0]
    imag_part = stacked[1]
    new_real = contract(real_part, cosine, axis_pos) - sign * contract(imag_part, sine, axis_pos)
    new_imag = contract(imag_part, cosine, axis_pos) + sign * contract(real_part, sine, axis_pos)
    return jnp.stack([new_real, new_imag])


def coulomb(zfreq, yfreq, xfreq, length, factor):

    def squared(index):
        signed = jnp.where(index > length // 2, index - length, index).astype(jnp.float32) * (
            2.0 * math.pi / length
        )
        return signed * signed

    total = (
        squared(zfreq)[:, None, None]
        + squared(yfreq)[None, :, None]
        + squared(xfreq)[None, None, :]
    )
    safe = jnp.where(total > 0, total, 1.0)
    return jnp.where(total > 0, 4.0 * math.pi * factor / safe, 0.0)


def per_device(orbitals, points):
    norbit, depth, rows, grid = orbitals.shape
    npoint = points.shape[0]
    slab_count = lax.axis_size("slab")
    wide_count = lax.axis_size("wide")
    slab_index = lax.axis_index("slab")
    wide_index = lax.axis_index("wide")
    cells = depth * rows * grid
    flat = orbitals.reshape(norbit, cells)
    zcoord = points // (grid * grid)
    ycoord = points // grid % grid
    xcoord = points % grid
    owned = (zcoord // depth == slab_index) & (ycoord // rows == wide_index)
    offset = ((zcoord - slab_index * depth) * rows + (ycoord - wide_index * rows)) * grid + xcoord
    offset = jnp.where(owned, offset, 0)
    picked = jnp.take(flat, offset, axis=1) * owned.astype(jnp.float32)[None, :]
    sampled = lax.psum(picked, ("slab", "wide"))
    correlation = jnp.dot(sampled.T, sampled, precision=highest)
    gram = correlation * correlation
    gram = gram + 0.01 * jnp.mean(jnp.diagonal(gram)) * jnp.eye(npoint, dtype=jnp.float32)
    factor = jnp.linalg.cholesky(gram)
    devices = slab_count * wide_count
    vectors = VEC_DEV * devices
    coeffs = jax.scipy.linalg.cho_solve((factor, True), jnp.eye(npoint, vectors, dtype=jnp.float32))
    coeff_rows = coeffs.T
    sampled_rows = sampled.T
    width = math.gcd(cells, 4096)

    def fit_block(turn, fitted):
        start = turn * width
        block = lax.dynamic_slice_in_dim(flat, start, width, 1)
        pairs = jnp.dot(sampled_rows, block, precision=highest)
        piece = jnp.dot(coeff_rows, pairs * pairs, precision=highest)
        return lax.dynamic_update_slice_in_dim(fitted, piece, start, 1)

    fitting = lax.fori_loop(0, cells // width, fit_block, jnp.zeros((vectors, cells), jnp.float32))
    cosine, sine = tables(grid)
    scale = 1.0 / float(grid * grid * grid)
    freqs = jnp.arange(grid, dtype=jnp.int32)
    stacked = fitting.reshape(2, vectors // 2, depth, rows, grid)
    spectrum = rotate(stacked, 3, -1.0, cosine, sine)
    spectrum = lax.all_to_all(spectrum, "wide", split_axis=1, concat_axis=3, tiled=True)
    spectrum = rotate(spectrum, 2, -1.0, cosine, sine)
    spectrum = lax.all_to_all(spectrum, "slab", split_axis=3, concat_axis=2, tiled=True)
    spectrum = rotate(spectrum, 1, -1.0, cosine, sine)
    block = grid // slab_count
    kernel = coulomb(
        freqs, slab_index * block + jnp.arange(block, dtype=jnp.int32), freqs, grid, scale
    )
    spectrum = spectrum * kernel
    spectrum = rotate(spectrum, 1, 1.0, cosine, sine)
    spectrum = lax.all_to_all(spectrum, "slab", split_axis=2, concat_axis=3, tiled=True)
    spectrum = rotate(spectrum, 2, 1.0, cosine, sine)
    spectrum = lax.all_to_all(spectrum, "wide", split_axis=3, concat_axis=1, tiled=True)
    spectrum = rotate(spectrum, 3, 1.0, cosine, sine)
    return spectrum.reshape(vectors, depth, rows, grid)


def solution(mesh):
    placed = (P(None, "slab", "wide", None), P())
    return jax.shard_map(
        per_device,
        mesh=mesh,
        in_specs=placed,
        out_specs=P(None, "slab", "wide", None),
        check_vma=False,
    )
```

profile of v0, /device:TPU:0, one launch (start us, length us, event | category | flops | bytes accessed | tf_op | source)
XLA Modules:
  0.0 1024.6 jit_solution(7619435522696950387)
XLA Ops:
  7.3 19.6 %copy.67 = f32[256,32,4,128]{0,3,2,1:T(8,128)} copy(f32[256,32,4,128]{3,2,1,0:T(4,128)} %param.4) | data formatting | bytes 33554432 | tf_op args[0]
  26.9 7.3 gather_fusion
  35.3 148.4 %all-reduce.3.cloned.1.call-done = f32[256,512]{0,1:T(8,128)} async-done(((f32[256,512]{0,1:T(8,128)}), f32[256,512]{0,1:T(8,128)}) %all-reduce.3.cloned.1.call-update) | async-done | bytes 524304 | tf_op jit(solution)/shard_map/psum | solution.py:70
  192.9 11.7 %cholesky.103 = f32[128,128]{1,0:T(8,128)S(1)} custom-call(f32[128,128]{1,0:T(8,128)S(1)} %cholesky.263), custom_call_target="Cholesky" | custom-call | tf_op jit(solution)/shard_map/jit(cholesky)/cholesky | solution.py:74
  204.7 9.8 custom-call.34
  215.2 11.7 %cholesky.215 = f32[128,128]{1,0:T(8,128)S(1)} custom-call(f32[128,128]{1,0:T(8,128)S(1)} %cholesky.267), custom_call_target="Cholesky" | custom-call | tf_op jit(solution)/shard_map/jit(cholesky)/cholesky | solution.py:74
  227.0 9.9 custom-call.35
  237.6 11.7 %cholesky.236 = f32[128,128]{1,0:T(8,128)S(1)} custom-call(f32[128,128]{1,0:T(8,128)S(1)} %cholesky.272), custom_call_target="Cholesky" | custom-call | tf_op jit(solution)/shard_map/jit(cholesky)/cholesky | solution.py:74
  250.0 9.8 custom-call.36
  260.5 11.7 %cholesky.253 = f32[128,128]{1,0:T(8,128)S(1)} custom-call(f32[128,128]{1,0:T(8,128)S(1)} %convolution_subtract_fusion.8), custom_call_target="Cholesky" | custom-call | tf_op jit(solution)/shard_map/jit(cholesky)/cholesky | solution.py:74
  276.3 10.6 %while.15 = (s32[]{:T(128)}, f32[512,512]{1,0:T(8,128)S(1)}, s32[4,2]{0,1:T(2,128)S(1)}, f32[4,128,128]{2,1,0:T(8,128)}, s32[]{:T(128)}) while((s32[]{:T(128)}, f32[512,512]{1,0:T(8,128)S(1)}, s32[4,2]{0,1:T(2,128)S(1)}, f32[4,128,128]{2,1,0:T(8,128)}, s32[]{:T(128)}) %tuple.60), condition=%wide.while_cond, body=%wide.while_body.sunk | while | flops 2 | bytes 132705 | solution.py:77
  286.8 40.3 %custom-call.37 = f32[4,128,128]{1,2,0:T(8,128)S(1)} custom-call(f32[4,128,128]{2,1,0:T(8,128)} %get-tuple-element.107), custom_call_target="InvertDiagBlocksLowerTriangular" | custom-call | tf_op jit(solution)/shard_map/jit(_cho_solve)/triangular_solve | solution.py:77
  335.0 68.7 %while.14 = (s32[]{:T(128)}, f32[128,16384]{0,1:T(8,128)}, f32[256,16384]{0,1:T(8,128)}, f32[512,256]{1,0:T(8,128)S(1)}, f32[128,512]{1,0:T(8,128)S(1)}, /*index=5*/s32[]{:T(128)}, s32[]{:T(128)}, s32[]{:T(128)}, s32[]{:T(128)}) while((s32[]{:T(128)}, f32[128,16384]{0,1:T(8,128)}, f32[256,16384]{0,1:T(8,128)}, f32[512,256]{1,0:T(8,128)S(1)}, ...), condition=%wide.region_11.12_spmd, body=%wide.region_10.11_spmd.sunk | while | flops 9665773568 | bytes 23855252 | solution.py:89
  335.0 9.1 fusion.295
  344.1 8.1 fusion.296
  352.2 9.1 fusion.295
  361.3 8.1 fusion.296
  369.3 9.1 fusion.295
  378.4 8.1 fusion.296
  386.5 9.1 fusion.295
  395.6 8.1 fusion.296
  403.7 13.2 %fusion.249 = (f32[64,16384]{0,1:T(8,128)}, f32[64,16384]{0,1:T(8,128)}) fusion(f32[128,16384]{0,1:T(8,128)} %get-tuple-element.99), kind=kLoop, calls=%fused_computation.325 | loop fusion | bytes 16777216 | tf_op jit(solution)/shard_map/slice | solution.py:30
  416.9 7.3 copy.72
  431.3 7.3 copy.74
  438.7 7.4 fusion.77
  457.7 101.2 %all_to_all.60 = f32[2,64,32,4,128]{4,2,3,0,1:T(8,128)} all-to-all(f32[2,64,32,4,128]{4,2,3,0,1:T(8,128)S(1)} %copy.77), channel_id=1, replica_groups=mesh['slab'=4,'wide'=32] {'wide'}, dimensions={1} | all-to-all | bytes 16777216 | tf_op jit(solution)/shard_map/all_to_all | solution.py:95
  558.9 12.2 %copy.150 = f32[2,32,2,32,4,128]{5,4,1,3,2,0:T(4,128)} copy(f32[2,32,2,32,4,128]{5,3,4,0,2,1:T(8,128)} %bitcast.268) | data formatting | bytes 16777216 | tf_op jit(solution)/shard_map/all_to_all | solution.py:95
  593.3 8.4 copy.83
  608.2 93.9 %all-to-all-done.1 = f32[2,2,32,128,128]{4,2,1,0,3:T(8,128)} async-done(((f32[2,2,32,128,128]{4,2,1,0,3:T(8,128)}), f32[2,2,32,128,128]{4,2,1,0,3:T(8,128)}, u32[]{:S(2)}, u32[]{:S(2)}) %all-to-all-start.1) | async-done | bytes 8388640 | tf_op jit(solution)/shard_map/all_to_all | solution.py:97
  751.7 97.3 %all_to_all.61 = f32[2,2,128,32,128]{4,3,1,0,2:T(8,128)S(1)} all-to-all(f32[2,2,128,32,128]{4,3,1,0,2:T(8,128)S(1)} %copy.93), channel_id=1, replica_groups=mesh['slab'=4,'wide'=32] {'slab'}, dimensions={2} | all-to-all | bytes 16777216 | tf_op jit(solution)/shard_map/all_to_all | solution.py:105
  876.2 102.6 %all_to_all.62 = f32[2,2,32,128,128]{4,2,1,0,3:T(8,128)S(1)} all-to-all(f32[2,2,32,128,128]{4,2,1,0,3:T(8,128)S(1)} %copy.99), channel_id=1, replica_groups=mesh['slab'=4,'wide'=32] {'wide'}, dimensions={3} | all-to-all | bytes 16777216 | tf_op jit(solution)/shard_map/all_to_all | solution.py:107
  1002.3 15.2 %copy.101 = f32[128,32,4,128]{3,2,1,0:T(4,128)} copy(f32[128,32,4,128]{3,1,2,0:T(8,128)} %bitcast.267) | data formatting | bytes 16777216 | tf_op jit(solution)/shard_map/reshape | solution.py:109
  (116 shorter events, 180.1 us)
Async XLA Ops:
  6.5 177.2 %all-reduce.3.cloned.1.call-start = ((), (), s32[]{:S(2)}) async-start(), calls=%async_computation.4 | async-start | bytes 1048576 | tf_op jit(solution)/shard_map/psum | solution.py:70
  331.3 3.7 copy-start.2
  438.6 7.4 copy-start.1
  438.7 7.4 copy-start.3
  446.0 4.0 copy-start
  601.8 100.3 %all-to-all-start.1 = ((f32[2,2,32,128,128]{4,2,1,0,3:T(8,128)}), f32[2,2,32,128,128]{4,2,1,0,3:T(8,128)}, u32[]{:S(2)}, u32[]{:S(2)}) async-start(f32[2,2,32,128,128]{4,2,1,0,3:T(8,128)} %copy.83), calls=%async_computation.1 | async-start | bytes 16777216 | tf_op jit(solution)/shard_map/all_to_all | solution.py:97
Sparse Core Ops, SparseCore 0:
  35.3 148.3 all-reduce.2
where the time goes:
time: 1030 us; the launch traced here: 1020 us
  blocking collectives  301 us (29%)
  waiting for transfers between devices  242 us (23%)
  matrix products  185 us (18%)
  local copies, waits for them, and re-layouts  139 us (13%)
  other arithmetic  133 us (13%)
  between operations  17.5 us (2%)
    psum x1, waiting for transfers between devices, per_device(): sampled = lax.psum(picked, ('slab', 'wide'))  148 us
    dot_general x24, matrix products, contract(): jnp.einsum(letters + ',' + letters[axis_pos] + 'k->' + target, values, ta...  109 us
    all_to_all x1, blocking collectives, per_device(): lax.all_to_all(spectrum, 'wide', split_axis=3, concat_axis=1, tiled=True)  103 us
    all_to_all x1, blocking collectives, per_device(): lax.all_to_all(spectrum, 'wide', split_axis=1, concat_axis=3, tiled=True)  101 us
    all_to_all x1, blocking collectives, per_device(): lax.all_to_all(spectrum, 'slab', split_axis=2, concat_axis=3, tiled=True)  97.3 us
    all_to_all x1, waiting for transfers between devices, per_device(): lax.all_to_all(spectrum, 'slab', split_axis=3, concat_axis=2, tiled=True)  93.9 us
    another operation x14, other arithmetic, per_device(): factor = jnp.linalg.cholesky(gram)  78.6 us
    another operation x3, other arithmetic, per_device(): jax.scipy.linalg.cho_solve((factor, True), jnp.eye(npoint, vectors, dtype...  40.4 us
  transfers between devices with their start and end apart: 2, of which 2 were waited for; matrix products, arithmetic and copies ran while one was open for 0% of the time, Pallas kernels for 0%

commit v1 on v0

v1 whole, which is shorter than its diff:
```python
import math

import jax
import jax.numpy as jnp
from jax import lax
from jax.sharding import PartitionSpec as P

AXES = ("slab", "wide")
highest = lax.Precision.HIGHEST
high = lax.Precision.HIGH


def hartley(length):
    index = jnp.arange(length, dtype=jnp.int32)
    phase = index[:, None] * index[None, :] % length
    angle = phase.astype(jnp.float32) * (2.0 * math.pi / length)
    return jnp.cos(angle) + jnp.sin(angle)


def coulomb(length, factor):
    index = jnp.arange(length, dtype=jnp.int32)
    signed = jnp.where(index > length // 2, index - length, index).astype(jnp.float32) * (
        2.0 * math.pi / length
    )
    squared = signed * signed
    total = squared[:, None, None] + squared[None, :, None] + squared[None, None, :]
    safe = jnp.where(total > 0, total, 1.0)
    return jnp.where(total > 0, 4.0 * math.pi * factor / safe, 0.0)


def exchange(blocks):
    return lax.all_to_all(blocks, AXES, split_axis=0, concat_axis=0, tiled=True)


def per_device(orbitals, points):
    norbit, depth, rows, grid = orbitals.shape
    npoint = points.shape[0]
    slab_count = lax.axis_size("slab")
    wide_count = lax.axis_size("wide")
    slab_index = lax.axis_index("slab")
    wide_index = lax.axis_index("wide")
    devices = slab_count * wide_count
    vectors = devices
    cells = depth * rows * grid
    flat = orbitals.reshape(norbit, cells)
    zcoord = points // (grid * grid)
    ycoord = points // grid % grid
    xcoord = points % grid
    owned = (zcoord // depth == slab_index) & (ycoord // rows == wide_index)
    offset = ((zcoord - slab_index * depth) * rows + (ycoord - wide_index * rows)) * grid + xcoord
    offset = jnp.where(owned, offset, 0)
    picked = jnp.take(flat, offset, axis=1) * owned.astype(jnp.float32)[None, :]
    mine = exchange(picked.T.reshape(devices, npoint // devices, norbit)).sum(0)
    sampled_rows = exchange(jnp.broadcast_to(mine[None], (devices,) + mine.shape))
    sampled_rows = sampled_rows.reshape(npoint, norbit)
    correlation = jnp.dot(sampled_rows, sampled_rows.T, precision=highest)
    gram = correlation * correlation
    gram = gram + 0.01 * jnp.mean(jnp.diagonal(gram)) * jnp.eye(npoint, dtype=jnp.float32)
    factor = jnp.linalg.cholesky(gram)
    coeffs = jax.scipy.linalg.cho_solve((factor, True), jnp.eye(npoint, vectors, dtype=jnp.float32))
    coeff_rows = coeffs.T
    width = math.gcd(cells, 4096)

    def fit_block(turn, fitted):
        start = turn * width
        block = lax.dynamic_slice_in_dim(flat, start, width, 1)
        pairs = jnp.dot(sampled_rows, block, precision=high)
        piece = jnp.dot(coeff_rows, pairs * pairs, precision=high)
        return lax.dynamic_update_slice_in_dim(fitted, piece, start, 1)

    fitting = lax.fori_loop(0, cells // width, fit_block, jnp.zeros((vectors, cells), jnp.float32))
    whole = exchange(fitting.reshape(vectors, depth, rows, grid))
    whole = whole.reshape(slab_count, wide_count, depth, rows, grid)
    xtab = hartley(grid)
    ytab = xtab.reshape(wide_count, rows, grid)
    ztab = xtab.reshape(slab_count, depth, grid)
    spec = jnp.einsum("swzyx,xk->swzyk", whole, xtab, precision=high)
    spec = jnp.einsum("swzyk,wyq->szqk", spec, ytab, precision=high)
    spec = jnp.einsum("szqk,szp->pqk", spec, ztab, precision=high)
    spec = spec * coulomb(grid, 1.0 / float(grid * grid * grid))
    spec = jnp.einsum("pqk,szp->szqk", spec, ztab, precision=high)
    spec = jnp.einsum("szqk,wyq->swzyk", spec, ytab, precision=high)
    spec = jnp.einsum("swzyk,xk->swzyx", spec, xtab, precision=high)
    return exchange(spec.reshape(devices, depth, rows, grid))


def solution(mesh):
    placed = (P(None, "slab", "wide", None), P())
    return jax.shard_map(
        per_device,
        mesh=mesh,
        in_specs=placed,
        out_specs=P(None, "slab", "wide", None),
        check_vma=False,
    )
```

time: 1030 us -> 573 us (0.56)
  blocking collectives: 301 us -> 131 us
  waiting for transfers between devices: 242 us -> 118 us
  matrix products: 185 us -> 105 us
  local copies, waits for them, and re-layouts: 139 us -> 78.9 us
  between operations: 17.5 us -> 3.88 us
  other arithmetic: 133 us -> 120 us
    all_to_all x3 -> x2, blocking collectives: 301 us -> 131 us  [exchange(): return lax.all_to_all(blocks, AXES, split_axis=0, concat_axis=0, tiled=True)]
    psum x1 -> x0, waiting for transfers between devices: 148 us -> none  [per_device(): sampled = lax.psum(picked, ('slab', 'wide'))]
    dot_general x33 -> x15, matrix products: 179 us -> 95.4 us  [the longest x4 21.6 us: fit_block(): pairs = jnp.dot(sampled_rows, block, precision=high)]
    all_to_all x1 -> x2, waiting for transfers between devices: 93.9 us -> 118 us  [exchange(): return lax.all_to_all(blocks, AXES, split_axis=0, concat_axis=0, tiled=True)]
    another operation x16 -> x12, local copies, waits for them, and re-layouts: 31 us -> 7.89 us  [the longest x4 20.4 us: rotate(): return jnp.stack([new_real, new_imag])]
    slice x5 -> x0, local copies, waits for them, and re-layouts: 22.8 us -> none  [rotate(): real_part = stacked[0]]
    all_to_all x4 -> x0, local copies, waits for them, and re-layouts: 19.4 us -> none  [the longest x1 12.2 us: per_device(): lax.all_to_all(spectrum, 'wide', split_axis=1, concat_axis=3, tiled=True)]
    squeeze x2 -> x0, local copies, waits for them, and re-layouts: 14.7 us -> none  [the longest x1 7.34 us: rotate(): real_part = stacked[0]]
where the time goes in v1:
time: 573 us; the launch traced here: 567 us
  blocking collectives  131 us (23%)
  other arithmetic  120 us (21%)
  waiting for transfers between devices  118 us (21%)
  matrix products  105 us (18%)
  local copies, waits for them, and re-layouts  78.9 us (14%)
  starting transfers between devices  10.5 us (2%)
    all_to_all x2, blocking collectives, exchange(): return lax.all_to_all(blocks, AXES, split_axis=0, concat_axis=0, tiled=True)  131 us
    all_to_all x2, waiting for transfers between devices, exchange(): return lax.all_to_all(blocks, AXES, split_axis=0, concat_axis=0, tiled=True)  118 us
    another operation x14, other arithmetic, per_device(): factor = jnp.linalg.cholesky(gram)  78.8 us
    another operation x3, other arithmetic, per_device(): jax.scipy.linalg.cho_solve((factor, True), jnp.eye(npoint, vectors, dtype...  39.6 us
    unnamed x4, local copies, waits for them, and re-layouts  28.4 us
    dot_general x4, matrix products, fit_block(): pairs = jnp.dot(sampled_rows, block, precision=high)  21.6 us
    dot_general x4, matrix products, fit_block(): piece = jnp.dot(coeff_rows, pairs * pairs, precision=high)  19 us
    reshape x1, local copies, waits for them, and re-layouts, per_device(): return exchange(spec.reshape(devices, depth, rows, grid))  14.9 us
  transfers between devices with their start and end apart: 2, of which 2 were waited for; matrix products, arithmetic and copies ran while one was open for 0% of the time, Pallas kernels for 0%

profile of v1, /device:TPU:0, one launch (start us, length us, event | category | flops | bytes accessed | tf_op | source)
XLA Modules:
  0.0 567.5 jit_solution(7049650729934695705)
XLA Ops:
  0.7 19.6 %copy.23 = f32[256,32,4,128]{0,3,2,1:T(8,128)} copy(f32[256,32,4,128]{3,2,1,0:T(4,128)} %param.4) | data formatting | bytes 33554432 | tf_op args[0]
  20.3 7.3 %gather_fusion = f32[512,256]{1,0:T(8,128)S(1)} fusion(f32[256,16384]{0,1:T(8,128)} %bitcast.120, s32[1024]{0:T(1024)S(1)} %pad_clamp_fusion), kind=kCustom, calls=%fused_computation | custom fusion | bytes 1050624 | tf_op jit(solution)/shard_map/jit(_take)/gather | solution.py:52
  28.0 24.7 %all_to_all.20 = f32[128,4,256]{2,1,0:T(4,128)S(1)} all-to-all(f32[128,4,256]{2,1,0:T(4,128)S(1)} %reshape.168), channel_id=1, replica_groups=mesh['slab'=4,'wide'=32] {'slab','wide'}, dimensions={0} | all-to-all | bytes 1048576 | tf_op jit(solution)/shard_map/all_to_all | solution.py:32
  58.4 13.6 %all-to-all-done.1 = f32[128,4,256]{2,1,0:T(4,128)S(1)} async-done(((f32[128,4,256]{2,1,0:T(4,128)}), f32[128,4,256]{2,1,0:T(4,128)S(1)}, u32[]{:S(2)}, u32[]{:S(2)}) %all-to-all-start.1) | async-done | bytes 524320 | tf_op jit(solution)/shard_map/all_to_all | solution.py:32
  80.8 11.7 %cholesky.103 = f32[128,128]{1,0:T(8,128)S(1)} custom-call(f32[128,128]{1,0:T(8,128)S(1)} %cholesky.263), custom_call_target="Cholesky" | custom-call | tf_op jit(solution)/shard_map/jit(cholesky)/cholesky | solution.py:59
  92.6 9.8 %custom-call.34 = f32[1,128,128]{1,2,0:T(8,128)S(1)} custom-call(f32[1,128,128]{2,1,0:T(8,128)S(1)} %get-tuple-element.160), custom_call_target="InvertDiagBlocksLowerTriangular" | custom-call | tf_op jit(solution)/shard_map/jit(cholesky)/cholesky | solution.py:59
  105.0 11.7 %cholesky.215 = f32[128,128]{1,0:T(8,128)S(1)} custom-call(f32[128,128]{1,0:T(8,128)S(1)} %cholesky.267), custom_call_target="Cholesky" | custom-call | tf_op jit(solution)/shard_map/jit(cholesky)/cholesky | solution.py:59
  116.7 10.2 %custom-call.35 = f32[1,128,128]{1,2,0:T(8,128)S(1)} custom-call(f32[1,128,128]{2,1,0:T(8,128)S(1)} %get-tuple-element.157), custom_call_target="InvertDiagBlocksLowerTriangular" | custom-call | tf_op jit(solution)/shard_map/jit(cholesky)/cholesky | solution.py:59
  128.5 11.7 %cholesky.236 = f32[128,128]{1,0:T(8,128)S(1)} custom-call(f32[128,128]{1,0:T(8,128)S(1)} %cholesky.272), custom_call_target="Cholesky" | custom-call | tf_op jit(solution)/shard_map/jit(cholesky)/cholesky | solution.py:59
  140.9 9.8 %custom-call.36 = f32[1,128,128]{1,2,0:T(8,128)S(1)} custom-call(f32[1,128,128]{2,1,0:T(8,128)S(1)} %get-tuple-element.154), custom_call_target="InvertDiagBlocksLowerTriangular" | custom-call | tf_op jit(solution)/shard_map/jit(cholesky)/cholesky | solution.py:59
  152.2 11.7 %cholesky.253 = f32[128,128]{1,0:T(8,128)S(1)} custom-call(f32[128,128]{1,0:T(8,128)S(1)} %convolution_subtract_fusion.8), custom_call_target="Cholesky" | custom-call | tf_op jit(solution)/shard_map/jit(cholesky)/cholesky | solution.py:59
  167.9 8.0 %while.15 = (s32[]{:T(128)}, f32[512,512]{1,0:T(8,128)S(1)}, s32[4,2]{0,1:T(2,128)S(1)}, f32[4,128,128]{2,1,0:T(8,128)S(1)}, s32[]{:T(128)}) while((s32[]{:T(128)}, f32[512,512]{1,0:T(8,128)S(1)}, s32[4,2]{0,1:T(2,128)S(1)}, f32[4,128,128]{2,1,0:T(8,128)S(1)}, s32[]{:T(128)}) %tuple.56), condition=%wide.while_cond, body=%wide.while_body.sunk | while | flops 2 | bytes 131181 | solution.py:60
  175.9 39.5 %custom-call.37 = f32[4,128,128]{1,2,0:T(8,128)S(1)} custom-call(f32[4,128,128]{2,1,0:T(8,128)S(1)} %get-tuple-element.107), custom_call_target="InvertDiagBlocksLowerTriangular" | custom-call | tf_op jit(solution)/shard_map/jit(_cho_solve)/triangular_solve | solution.py:60
  223.2 40.6 %while.14 = (s32[]{:T(128)}, f32[128,16384]{0,1:T(8,128)}, f32[256,16384]{0,1:T(8,128)}, f32[512,256]{1,0:T(8,128)S(1)}, f32[128,512]{1,0:T(8,128)S(1)}, /*index=5*/s32[]{:T(128)}, s32[]{:T(128)}, s32[]{:T(128)}, s32[]{:T(128)}) while((s32[]{:T(128)}, f32[128,16384]{0,1:T(8,128)}, f32[256,16384]{0,1:T(8,128)}, f32[512,256]{1,0:T(8,128)S(1)}, ...), condition=%wide.region_11.12_spmd, body=%wide.region_10.11_spmd.sunk | while | flops 4833935360 | bytes 23855252 | solution.py:71
  223.2 5.4 fusion.176
  228.6 4.8 fusion.177
  233.4 5.4 fusion.176
  238.8 4.8 fusion.177
  243.5 5.4 fusion.176
  253.7 5.4 fusion.176
  259.1 4.8 fusion.177
  263.9 10.3 %copy.27 = f32[128,32,4,128]{3,2,1,0:T(4,128)} copy(f32[128,32,4,128]{0,3,2,1:T(8,128)} %bitcast.20) | data formatting | bytes 16777216 | tf_op jit(solution)/shard_map/reshape | solution.py:72
  274.1 5.9 %all-to-all-start.2 = ((f32[128,32,4,128]{3,2,1,0:T(4,128)}), f32[128,32,4,128]{3,2,1,0:T(4,128)}, u32[]{:S(2)}, u32[]{:S(2)}) async-start(f32[128,32,4,128]{3,2,1,0:T(4,128)} %copy.27), calls=%async_computation.2 | async-start | bytes 16777216 | tf_op jit(solution)/shard_map/all_to_all | solution.py:32
  280.2 104.6 %all-to-all-done.2 = f32[128,32,4,128]{3,2,1,0:T(4,128)} async-done(((f32[128,32,4,128]{3,2,1,0:T(4,128)}), f32[128,32,4,128]{3,2,1,0:T(4,128)}, u32[]{:S(2)}, u32[]{:S(2)}) %all-to-all-start.2) | async-done | bytes 8388640 | tf_op jit(solution)/shard_map/all_to_all | solution.py:32
  384.8 13.9 %fusion.21 = f32[4,32,32,4,128]{4,1,3,2,0:T(8,128)S(1)} fusion(f32[4,32,32,4,128]{4,3,2,1,0:T(4,128)} %bitcast.21), kind=kOutput, calls=%fused_computation.21 | convolution fusion | flops 1610858496 | bytes 16777216 | tf_op jit(solution)/shard_map/swzyx,xk->swzyk/dot_general | solution.py:77
  403.4 8.9 %fusion.26 = f32[128,128,128,1]{2,0,3,1:T(8,128)S(1)} fusion(f32[4,32,128,128]{3,2,1,0:T(8,128)S(1)} %convolution_bitcast_fusion, s32[4,32]{1,0:T(4,128)S(1)} %multiply_add_fusion), kind=kOutput, calls=%fused_computation.26 | convolution fusion | flops 1610858496 | bytes 16777728 | tf_op jit(solution)/shard_map/szqk,szp->pqk/dot_general | solution.py:79
  412.3 6.2 %fusion.14 = f32[4,32,128,128]{3,1,2,0:T(8,128)S(1)} fusion(f32[128,128,128,1]{2,0,3,1:T(8,128)S(1)} %fusion.26, f32[128]{0:T(128)S(1)} %fusion.122, f32[128,128]{0,1:T(8,128)S(1)} %broadcast_add_fusion, s32[4,32]{1,0:T(4,128)S(1)} %multiply_add_fusion), kind=kOutput, calls=%fused_computation.16 | convolution fusion | flops 1623441408 | bytes 16843776 | tf_op jit(solution)/shard_map/pqk,szp->szqk/dot_general | solution.py:81
  418.5 8.9 %fusion.33 = f32[4,32,32,4,128]{4,1,2,0,3:T(8,128)S(1)} fusion(f32[4,32,128,128]{3,1,2,0:T(8,128)S(1)} %fusion.14, s32[32,4]{0,1:T(4,128)S(1)} %multiply_add_fusion.1), kind=kOutput, calls=%fused_computation.33 | convolution fusion | flops 1610858496 | bytes 16777728 | tf_op jit(solution)/shard_map/szqk,wyq->swzyk/dot_general | solution.py:82
  427.4 11.2 %fusion.23 = f32[4,32,32,4,128]{4,2,3,1,0:T(8,128)} fusion(f32[4,32,32,4,128]{4,1,2,0,3:T(8,128)S(1)} %fusion.33), kind=kOutput, calls=%fused_computation.23 | convolution fusion | flops 1610858496 | bytes 16777216 | tf_op jit(solution)/shard_map/swzyk,xk->swzyx/dot_general | solution.py:83
  438.6 14.9 %copy.33 = f32[128,32,4,128]{3,2,1,0:T(4,128)} copy(f32[128,32,4,128]{3,1,2,0:T(8,128)} %bitcast.123) | data formatting | bytes 16777216 | tf_op jit(solution)/shard_map/reshape | solution.py:84
  453.4 105.9 %all_to_all.21 = f32[128,32,4,128]{3,2,1,0:T(4,128)} all-to-all(f32[128,32,4,128]{3,2,1,0:T(4,128)} %copy.33), channel_id=1, replica_groups=mesh['slab'=4,'wide'=32] {'slab','wide'}, dimensions={0} | all-to-all | bytes 16777216 | tf_op jit(solution)/shard_map/all_to_all | solution.py:32
  559.3 7.9 %copy.79 = f32[128,32,4,128]{3,2,1,0:T(4,128)} copy(f32[128,32,4,128]{3,2,1,0:T(4,128)} %all_to_all.21) | data formatting | bytes 16777216
  (75 shorter events, 47.9 us)
Async XLA Ops:
  53.7 18.3 %all-to-all-start.1 = ((f32[128,4,256]{2,1,0:T(4,128)}), f32[128,4,256]{2,1,0:T(4,128)S(1)}, u32[]{:S(2)}, u32[]{:S(2)}) async-start(f32[128,4,256]{2,1,0:T(4,128)} %broadcast_in_dim.44), calls=%async_computation.1 | async-start | bytes 1048576 | tf_op jit(solution)/shard_map/all_to_all | solution.py:32
  79.8 1.0 copy-start
  274.1 110.6 %all-to-all-start.2 = ((f32[128,32,4,128]{3,2,1,0:T(4,128)}), f32[128,32,4,128]{3,2,1,0:T(4,128)}, u32[]{:S(2)}, u32[]{:S(2)}) async-start(f32[128,32,4,128]{3,2,1,0:T(4,128)} %copy.27), calls=%async_computation.2 | async-start | bytes 16777216 | tf_op jit(solution)/shard_map/all_to_all | solution.py:32

commit v2 on v1

v2 whole, which is shorter than its diff:
```python
import functools
import math

import jax
import jax.numpy as jnp
from jax import lax
from jax.experimental import pallas as pl
from jax.experimental.pallas import tpu as pltpu
from jax.sharding import PartitionSpec as P

AXES = ("slab", "wide")
HI = lax.Precision.HIGHEST
BLK = 128
CHUNKS = 2
SLOTS = 8


def hartley(length):
    index = jnp.arange(length, dtype=jnp.int32)
    phase = index[:, None] * index[None, :] % length
    angle = phase.astype(jnp.float32) * (2.0 * math.pi / length)
    return jnp.cos(angle) + jnp.sin(angle)


def exchange(blocks):
    return lax.all_to_all(blocks, AXES, split_axis=0, concat_axis=0, tiled=True)


def halves(value):
    top = value.astype(jnp.bfloat16)
    return top, (value - top.astype(jnp.float32)).astype(jnp.bfloat16)


def split(value):
    top = lax.reduce_precision(value, exponent_bits=8, mantissa_bits=7)
    return top.astype(jnp.bfloat16), (value - top).astype(jnp.bfloat16)


def mul3(left, right):
    def one(a, b):
        return jnp.dot(a, b, preferred_element_type=jnp.float32)

    return one(left[0], right[0]) + (one(left[1], right[0]) + one(left[0], right[1]))


def whole_spec():
    return pl.BlockSpec(memory_space=pltpu.VMEM)


def pick_kernel(info, orb, out_ref, buf, acc, order, sems):
    npoint = info.shape[1]
    lane = lax.broadcasted_iota(jnp.int32, (acc.shape[0], BLK), 1)
    acc[...] = jnp.zeros_like(acc)

    def collect(m, count):
        order[count] = m
        return count + info[0, m]

    total = lax.fori_loop(0, npoint, collect, 0)

    def copy(i):
        m = order[i]
        slot = i % SLOTS
        return pltpu.make_async_copy(orb.at[:, info[1, m]], buf.at[slot], sems.at[slot])

    @pl.loop(0, jnp.minimum(total, SLOTS - 1))
    def _(i):
        copy(i).start()

    @pl.loop(0, total)
    def _(i):
        @pl.when(i + SLOTS - 1 < total)
        def _():
            copy(i + SLOTS - 1).start()

        copy(i).wait()
        m = order[i]
        slot = i % SLOTS
        line = buf[slot, :, info[2, m], :]
        moved = pltpu.roll(line, (m + BLK - info[3, m]) % BLK, 1)
        spot = pl.multiple_of(m // BLK * BLK, BLK)
        acc[:, pl.ds(spot, BLK)] = jnp.where(lane == m % BLK, moved, acc[:, pl.ds(spot, BLK)])

    out_ref[...] = acc[...].T


def pick(info, orbitals):
    norbit, depth, rows, grid = orbitals.shape
    npoint = info.shape[1]
    return pl.pallas_call(
        pick_kernel,
        out_shape=jax.ShapeDtypeStruct((npoint, norbit), jnp.float32),
        in_specs=[pl.BlockSpec(memory_space=pltpu.SMEM), pl.BlockSpec(memory_space=pl.ANY)],
        out_specs=whole_spec(),
        scratch_shapes=[
            pltpu.VMEM((SLOTS, norbit, rows, grid), jnp.float32),
            pltpu.VMEM((norbit, npoint), jnp.float32),
            pltpu.SMEM((npoint + 1,), jnp.int32),
            pltpu.SemaphoreType.DMA((SLOTS,)),
        ],
        name="pick",
    )(info, orbitals)


def factor_block(tile):
    lane = lax.broadcasted_iota(jnp.int32, (8, BLK), 1)
    sub = lax.broadcasted_iota(jnp.int32, (8, BLK), 0)
    groups = [tile[8 * i : 8 * i + 8, :] for i in range(BLK // 8)]
    for k in range(BLK):
        here, off = k // 8, k % 8
        row = jnp.broadcast_to(groups[here][off : off + 1, :], (8, BLK))
        piv = jnp.broadcast_to(row[:, k : k + 1], (8, BLK))
        inv = 1.0 / piv
        unit = jnp.where(lane == k, 1.0, row)
        scaled = unit * inv
        for i in range(here, BLK // 8):
            g = groups[i]
            col = jnp.broadcast_to(g[:, k : k + 1], (8, BLK))
            if i == here:
                col = jnp.where(sub > off, col, 0.0)
                base = jnp.where((lane == k) & (sub > off), 0.0, g)
            else:
                base = jnp.where(lane == k, 0.0, g)
            groups[i] = base - col * scaled
    return jnp.concatenate(groups, axis=0)

def coeff_kernel(s_ref, out_ref, g_ref, p_ref, l_ref):
    n = s_ref.shape[0]
    nb = n // BLK
    rows = s_ref[...]
    corr = lax.dot_general(rows, rows, (((1,), (1,)), ((), ())), precision=HI, preferred_element_type=jnp.float32)
    gram = corr * corr
    r = lax.broadcasted_iota(jnp.int32, (n, n), 0)
    c = lax.broadcasted_iota(jnp.int32, (n, n), 1)
    mean = jnp.sum(jnp.where(r == c, gram, 0.0)) * (1.0 / n)
    g_ref[...] = gram + jnp.where(r == c, 0.01 * mean, 0.0)
    rr = lax.broadcasted_iota(jnp.int32, (BLK, BLK), 0)
    cc = lax.broadcasted_iota(jnp.int32, (BLK, BLK), 1)

    def step(t, carry):
        start = pl.multiple_of((nb - 1 - t) * BLK, BLK)
        tile = factor_block(g_ref[pl.ds(start, BLK), pl.ds(start, BLK)])
        diag = jnp.sum(jnp.where(rr == cc, tile, 0.0), axis=1, keepdims=True)
        low = jnp.where(cc < rr, tile, jnp.where(rr == cc, 1.0, 0.0)) * lax.rsqrt(diag)
        l_ref[pl.ds(start, BLK), :] = low
        panel = jnp.dot(low, g_ref[pl.ds(start, BLK), :], precision=HI, preferred_element_type=jnp.float32)
        p_ref[pl.ds(start, BLK), :] = panel

        @pl.when(t < nb - 1)
        def _():
            g_ref[...] -= lax.dot_general(panel, panel, (((0,), (0,)), ((), ())), precision=HI, preferred_element_type=jnp.float32)
        return carry

    lax.fori_loop(0, nb, step, 0)
    first = l_ref[0:BLK, :]
    out_ref[:, 0:BLK] = lax.dot_general(first, first, (((0,), (0,)), ((), ())), precision=HI, preferred_element_type=jnp.float32)
    for b in range(1, nb):
        lo = b * BLK
        part = lax.dot_general(out_ref[:, 0:lo], p_ref[lo : lo + BLK, 0:lo], (((1,), (1,)), ((), ())), precision=HI, preferred_element_type=jnp.float32)
        out_ref[:, lo : lo + BLK] = -jnp.dot(part, l_ref[lo : lo + BLK, :], precision=HI, preferred_element_type=jnp.float32)

def coefficients(rows):
    n = rows.shape[0]
    return pl.pallas_call(
        coeff_kernel,
        out_shape=jax.ShapeDtypeStruct((BLK, n), jnp.float32),
        scratch_shapes=[pltpu.VMEM((n, n), jnp.float32), pltpu.VMEM((n, n), jnp.float32), pltpu.VMEM((n, BLK), jnp.float32)],
        name="coefficients",
    )(rows)


def fit_kernel(sh, sl, ch, cl, orb, out_ref, bh, bl):
    lines = orb.shape[1]
    for r in range(lines):
        top, low = halves(orb[:, r, :])
        bh[:, r * BLK : (r + 1) * BLK] = top
        bl[:, r * BLK : (r + 1) * BLK] = low
    for r in range(0, lines, 4):
        cut = slice(r * BLK, (r + 4) * BLK)
        pairs = mul3((sh[...], sl[...]), (bh[:, cut], bl[:, cut]))
        piece = mul3((ch[...], cl[...]), halves(pairs * pairs))
        for k in range(4):
            out_ref[:, r + k, :] = piece[:, k * BLK : (k + 1) * BLK]


def fit(sampled, coeffs, orbitals, first, count, lines=8):
    norbit, total, grid = orbitals.shape
    vectors, npoint = coeffs[0].shape
    start = first // lines
    return pl.pallas_call(
        fit_kernel,
        out_shape=jax.ShapeDtypeStruct((vectors, count, grid), jnp.float32),
        grid=(count // lines,),
        in_specs=[
            pl.BlockSpec((npoint, norbit), lambda i: (0, 0)),
            pl.BlockSpec((npoint, norbit), lambda i: (0, 0)),
            pl.BlockSpec((vectors, npoint), lambda i: (0, 0)),
            pl.BlockSpec((vectors, npoint), lambda i: (0, 0)),
            pl.BlockSpec((norbit, lines, grid), lambda i: (0, start + i, 0)),
        ],
        out_specs=pl.BlockSpec((vectors, lines, grid), lambda i: (0, i, 0)),
        scratch_shapes=[
            pltpu.VMEM((norbit, lines * grid), jnp.bfloat16),
            pltpu.VMEM((norbit, lines * grid), jnp.bfloat16),
        ],
        cost_estimate=pl.CostEstimate(
            flops=6 * count * grid * npoint * (norbit + vectors),
            transcendentals=0,
            bytes_accessed=4 * count * grid * (norbit + vectors),
        ),
        name="fit",
    )(*sampled, *coeffs, orbitals)


def planes_in_kernel(xh, xl, yh, yl, in_ref, out_ref):
    for pair in range(in_ref.shape[2] // 8):
        tile = in_ref[0, :, 8 * pair : 8 * pair + 8, :].reshape(2 * BLK, BLK)
        along = mul3(halves(tile), (xh[...], xl[...]))
        both = mul3((yh[...], yl[...]), halves(along))
        out_ref[0, 2 * pair] = both[:BLK]
        out_ref[0, 2 * pair + 1] = both[BLK:]


def planes_out_kernel(xh, xl, yh, yl, in_ref, out_ref):
    for pair in range(in_ref.shape[1] // 2):
        tile = jnp.concatenate([in_ref[0, 2 * pair], in_ref[0, 2 * pair + 1]], axis=0)
        both = mul3((yh[...], yl[...]), halves(tile))
        along = mul3(halves(both), (xh[...], xl[...]))
        out_ref[0, :, 8 * pair : 8 * pair + 8, :] = along.reshape(32, 8, BLK)


def planes(kernel, xtab, ytab, values, out_shape, name, step=8):
    slabs, depth = (values.shape[0], values.shape[2] // 4) if name == "planes_in" else values.shape[:2]
    cellwise = pl.BlockSpec((1, 32, 4 * step, BLK), lambda s, i: (s, 0, i, 0))
    planewise = pl.BlockSpec((1, step, BLK, BLK), lambda s, i: (s, i, 0, 0))
    small = pl.BlockSpec((BLK, BLK), lambda s, i: (0, 0))
    large = pl.BlockSpec((2 * BLK, 2 * BLK), lambda s, i: (0, 0))
    inward = name == "planes_in"
    return pl.pallas_call(
        kernel,
        out_shape=jax.ShapeDtypeStruct(out_shape, jnp.float32),
        grid=(slabs, depth // step),
        in_specs=[small, small, large, large, cellwise if inward else planewise],
        out_specs=planewise if inward else cellwise,
        cost_estimate=pl.CostEstimate(
            flops=6 * values.size * 3 * BLK, transcendentals=0, bytes_accessed=8 * values.size
        ),
        name=name,
    )(*xtab, *ytab, values)


def columns_kernel(count, zh, zl, *refs):
    ins, outs = refs[:count], refs[count:]
    lines = ins[0].shape[1]
    base = pl.program_id(0) * lines
    length = BLK
    unit = 2.0 * math.pi / length

    def square(index):
        signed = jnp.where(index > length // 2, index - length, index).astype(jnp.float32) * unit
        return signed * signed

    zsq = square(lax.broadcasted_iota(jnp.int32, (BLK, BLK), 0))
    xsq = square(lax.broadcasted_iota(jnp.int32, (BLK, BLK), 1))
    flat = zsq + xsq
    part = BLK // count
    for j in range(0, lines, 2):
        tile = jnp.concatenate(
            [
                jnp.concatenate([ref[:, j, :] for ref in ins], axis=0),
                jnp.concatenate([ref[:, j + 1, :] for ref in ins], axis=0),
            ],
            axis=1,
        )
        spec = mul3((zh[0], zl[0]), halves(tile))
        weights = []
        for k in range(2):
            index = base + j + k
            total = flat + square(jnp.full((BLK, BLK), index, jnp.int32))
            safe = jnp.where(total > 0, total, 1.0)
            scale = 4.0 * math.pi / float(length**3)
            weights.append(jnp.where(total > 0, scale / safe, 0.0))
        spec = spec * jnp.concatenate(weights, axis=1)
        back = mul3((zh[1], zl[1]), halves(spec))
        for c, ref in enumerate(outs):
            for k in range(2):
                ref[:, j + k, :] = back[c * part : (c + 1) * part, k * BLK : (k + 1) * BLK]


def columns(ztab, values, lines=8):
    count = len(values)
    part = BLK // count
    spec = pl.BlockSpec((part, lines, BLK), lambda i: (0, i, 0))
    table = pl.BlockSpec((2, BLK, BLK), lambda i: (0, 0, 0))
    size = BLK**3
    return pl.pallas_call(
        functools.partial(columns_kernel, count),
        out_shape=[jax.ShapeDtypeStruct((part, BLK, BLK), jnp.float32)] * count,
        grid=(BLK // lines,),
        in_specs=[table, table] + [spec] * count,
        out_specs=[spec] * count,
        cost_estimate=pl.CostEstimate(
            flops=12 * size * BLK, transcendentals=size, bytes_accessed=8 * size
        ),
        name="columns",
    )(*ztab, *values)


def per_device(orbitals, points):
    norbit, depth, rows, grid = orbitals.shape
    npoint = points.shape[0]
    slabs = lax.axis_size("slab")
    wides = lax.axis_size("wide")
    slab_index = lax.axis_index("slab")
    wide_index = lax.axis_index("wide")
    devices = slabs * wides
    zcoord = points // (grid * grid)
    ycoord = points // grid % grid
    xcoord = points % grid
    owned = (zcoord // depth == slab_index) & (ycoord // rows == wide_index)
    info = jnp.stack([owned.astype(jnp.int32), zcoord % depth, ycoord % rows, xcoord])
    picked = pick(info, orbitals)
    mine = exchange(picked.reshape(devices, npoint // devices, norbit)).sum(0)
    sampled_rows = exchange(jnp.broadcast_to(mine[None], (devices,) + mine.shape))
    sampled_rows = sampled_rows.reshape(npoint, norbit)
    coeffs = split(coefficients(sampled_rows))
    sampled = split(sampled_rows)

    table = hartley(grid)
    xtab = split(table)
    part = depth // CHUNKS
    lines = table.reshape(grid, wides, 1, rows)
    eye = jnp.eye(2, dtype=jnp.float32)
    ysplit = (eye[:, None, None, :, None] * lines[None]).reshape(2 * grid, wides * 2 * rows)
    ztable = table.reshape(grid, slabs, CHUNKS, part).transpose(0, 2, 1, 3).reshape(grid, grid)
    yin, yout = split(ysplit), split(ysplit.T)
    ztab = split(jnp.stack([ztable, ztable.T]))

    flat = orbitals.reshape(norbit, depth * rows, grid)
    spectra = []
    for c in range(CHUNKS):
        piece = fit(sampled, coeffs, flat, c * part * rows, part * rows)
        whole = exchange(piece).reshape(slabs, wides, part * rows, grid)
        spec = planes(planes_in_kernel, xtab, yin, whole, (slabs, part, grid, grid), "planes_in")
        spectra.append(spec.reshape(slabs * part, grid, grid))
    spectra = columns(ztab, spectra)
    out = []
    for c in range(CHUNKS):
        spec = spectra[c].reshape(slabs, part, grid, grid)
        back = planes(planes_out_kernel, xtab, yout, spec, (slabs, wides, part * rows, grid), "planes_out")
        out.append(exchange(back.reshape(devices, part * rows, grid)).reshape(devices, part, rows, grid))
    return jnp.concatenate(out, axis=1)


def solution(mesh):
    placed = (P(None, "slab", "wide", None), P())
    return jax.shard_map(
        per_device,
        mesh=mesh,
        in_specs=placed,
        out_specs=P(None, "slab", "wide", None),
        check_vma=False,
    )
```

time: 573 us -> 469 us (0.82)
  Pallas kernels: 0 us -> 239 us
  matrix products: 105 us -> 0 us
  other arithmetic: 120 us -> 20.4 us
  local copies, waits for them, and re-layouts: 78.9 us -> 3.83 us
  blocking collectives: 131 us -> 97.9 us
  waiting for transfers between devices: 118 us -> 88.8 us
  starting transfers between devices: 10.5 us -> 17.9 us
    pallas_call x0 -> x9, Pallas kernels: none -> 239 us  [the longest x1 77.7 us: coefficients(): pl.pallas_call(coeff_kernel, out_shape=jax.ShapeDtypeStruct((BLK, n), jnp...]
    another operation x17 -> x2, other arithmetic: 118 us -> 1.32 us  [per_device(): jnp.stack([owned.astype(jnp.int32), zcoord % depth, ycoord % rows, xcoord])]
    dot_general x15 -> x0, matrix products: 95.4 us -> none  [the longest x4 21.6 us: fit_block(): pairs = jnp.dot(sampled_rows, block, precision=high)]
    all_to_all x2 -> x3, blocking collectives: 131 us -> 97.9 us  [exchange(): return lax.all_to_all(blocks, AXES, split_axis=0, concat_axis=0, tiled=True)]
    all_to_all x2 -> x3, waiting for transfers between devices: 118 us -> 88.8 us  [exchange(): return lax.all_to_all(blocks, AXES, split_axis=0, concat_axis=0, tiled=True)]
    unnamed x4 -> x0, local copies, waits for them, and re-layouts: 28.4 us -> none
    reshape x3 -> x1, local copies, waits for them, and re-layouts: 25.3 us -> 1.19 us  [per_device(): mine = exchange(picked.reshape(devices, npoint // devices, norbit)).sum(0)]
    gather x2 -> x0, local copies, waits for them, and re-layouts: 12 us -> none  [the longest x1 7.34 us: per_device(): picked = jnp.take(flat, offset, axis=1) * owned.astype(jnp.float32)[None, :]]
  transfers between devices with their start and end apart: 2 -> 3, of which waited for: 2 -> 3; matrix products, arithmetic and copies ran while one was open for 0% -> 1% of each run, Pallas kernels for 0% -> 14%
where the time goes in v2:
time: 469 us; the launch traced here: 468 us
  Pallas kernels  239 us (51%)
  blocking collectives  97.9 us (21%)
  waiting for transfers between devices  88.8 us (19%)
  other arithmetic  20.4 us (4%)
  starting transfers between devices  17.9 us (4%)
    all_to_all x3, blocking collectives, exchange(): return lax.all_to_all(blocks, AXES, split_axis=0, concat_axis=0, tiled=True)  97.9 us
    all_to_all x3, waiting for transfers between devices, exchange(): return lax.all_to_all(blocks, AXES, split_axis=0, concat_axis=0, tiled=True)  88.8 us
    pallas_call x1, Pallas kernels, coefficients(): pl.pallas_call(coeff_kernel, out_shape=jax.ShapeDtypeStruct((BLK, n), jnp...  77.7 us
    pallas_call x2, Pallas kernels, fit(): pl.pallas_call(fit_kernel, out_shape=jax.ShapeDtypeStruct((vectors, count...  76 us
    pallas_call x4, Pallas kernels, planes(): pl.pallas_call(kernel, out_shape=jax.ShapeDtypeStruct(out_shape, jnp.floa...  55.3 us
    pallas_call x1, Pallas kernels, columns(): pl.pallas_call(functools.partial(columns_kernel, count), out_shape=[jax.S...  19.2 us
    all_to_all x3, starting transfers between devices, exchange(): return lax.all_to_all(blocks, AXES, split_axis=0, concat_axis=0, tiled=True)  17.9 us
    pallas_call x1, Pallas kernels, pick(): pl.pallas_call(pick_kernel, out_shape=jax.ShapeDtypeStruct((npoint, norbi...  11.3 us
  transfers between devices with their start and end apart: 3, of which 3 were waited for; matrix products, arithmetic and copies ran while one was open for 1% of the time, Pallas kernels for 14%

profile of v2, /device:TPU:0, one launch (start us, length us, event | category | flops | bytes accessed | tf_op | source)
XLA Modules:
  0.0 468.3 jit_solution(3796871552437686848)
XLA Ops:
  0.0 0.7 add_select_fusion.6
  0.7 0.7 and_convert_fusion
  1.4 0.6 pad_add_fusion.info
  2.0 11.3 %pick.1 = f32[512,256]{1,0:T(8,128)} custom-call(s32[4,512]{1,0:T(4,128)} %pad_add_fusion.info, f32[256,32,4,128]{3,2,1,0:T(4,128)} %orb.1), custom_call_target="tpu_custom_call" | custom-call | tf_op jit(solution)/shard_map/pick/pallas_call | solution.py:90
  13.3 1.2 reshape.190
  14.5 20.5 %all_to_all.30 = f32[128,4,256]{2,1,0:T(4,128)S(1)} all-to-all(f32[128,4,256]{2,1,0:T(4,128)S(1)} %reshape.190), channel_id=1, replica_groups=mesh['slab'=4,'wide'=32] {'slab','wide'}, dimensions={0} | all-to-all | bytes 1048576 | tf_op jit(solution)/shard_map/all_to_all | solution.py:26
  35.2 18.1 %all_to_all.31 = f32[128,4,256]{2,1,0:T(4,128)S(1)} all-to-all(f32[128,4,256]{2,1,0:T(4,128)S(1)} %broadcast_in_dim.2), channel_id=1, replica_groups=mesh['slab'=4,'wide'=32] {'slab','wide'}, dimensions={0} | all-to-all | bytes 1048576 | tf_op jit(solution)/shard_map/all_to_all | solution.py:26
  53.3 1.0 reshape.191.s_ref
  54.3 77.7 %coefficients.1 = f32[128,512]{1,0:T(8,128)} custom-call(f32[512,256]{1,0:T(8,128)} %reshape.191.s_ref), custom_call_target="tpu_custom_call" | custom-call | tf_op jit(solution)/shard_map/coefficients/pallas_call | solution.py:164
  132.0 1.9 fusion
  133.9 1.7 fusion.3
  135.6 38.0 %fit.3 = f32[128,64,128]{2,1,0:T(8,128)} custom-call(bf16[512,256]{1,0:T(8,128)(2,1)} %get-tuple-element.12.sh, bf16[512,256]{1,0:T(8,128)(2,1)} %get-tuple-element.11.sl, bf16[128,512]{1,0:T(8,128)(2,1)} %get-tuple-element.14.ch, bf16[128,512]{1,0:T(8,128)(2,1)} %get-tuple-element.13.cl, f32[256,128,128]{2,1,0:T(8,128)} %bitcast.33), custom_call_target="tpu_custom_call" | custom-call | flops 9663676416 | bytes 12582912 | tf_op jit(solution)/shard_map/fit/pallas_call | solution.py:190
  173.6 6.0 %all-to-all-start.3 = ((f32[128,64,128]{2,1,0:T(8,128)}), f32[128,64,128]{2,1,0:T(8,128)}, u32[]{:S(2)}, u32[]{:S(2)}) async-start(f32[128,64,128]{2,1,0:T(8,128)} %fit.3), calls=%async_computation.3 | async-start | bytes 8388608 | tf_op jit(solution)/shard_map/all_to_all | solution.py:26
  179.6 37.9 %fit.2 = f32[128,64,128]{2,1,0:T(8,128)} custom-call(bf16[512,256]{1,0:T(8,128)(2,1)} %get-tuple-element.12.sh, bf16[512,256]{1,0:T(8,128)(2,1)} %get-tuple-element.11.sl, bf16[128,512]{1,0:T(8,128)(2,1)} %get-tuple-element.14.ch, bf16[128,512]{1,0:T(8,128)(2,1)} %get-tuple-element.13.cl, f32[256,128,128]{2,1,0:T(8,128)} %bitcast.34), custom_call_target="tpu_custom_call" | custom-call | flops 9663676416 | bytes 12582912 | tf_op jit(solution)/shard_map/fit/pallas_call | solution.py:190
  217.6 15.2 %all-to-all-done.3 = f32[128,64,128]{2,1,0:T(8,128)} async-done(((f32[128,64,128]{2,1,0:T(8,128)}), f32[128,64,128]{2,1,0:T(8,128)}, u32[]{:S(2)}, u32[]{:S(2)}) %all-to-all-start.3) | async-done | bytes 4194336 | tf_op jit(solution)/shard_map/all_to_all | solution.py:26
  232.8 5.8 %all-to-all-start.2 = ((f32[128,64,128]{2,1,0:T(8,128)}), f32[128,64,128]{2,1,0:T(8,128)}, u32[]{:S(2)}, u32[]{:S(2)}) async-start(f32[128,64,128]{2,1,0:T(8,128)} %fit.2), calls=%async_computation.2 | async-start | bytes 8388608 | tf_op jit(solution)/shard_map/all_to_all | solution.py:26
  238.7 0.6 sine_add_fusion.2
  239.5 0.8 copy.4.yl
  240.3 0.8 copy.3.yh
  241.0 0.9 reduce-precision_convert_fusion.5
  242.5 0.7 fusion.4
  243.2 0.7 fusion.1
  243.9 15.2 %planes_in.3 = f32[4,16,128,128]{3,2,1,0:T(8,128)} custom-call(bf16[128,128]{1,0:T(8,128)(2,1)} %get-tuple-element.25.xh, bf16[128,128]{1,0:T(8,128)(2,1)} %get-tuple-element.26.xl, bf16[256,256]{1,0:T(8,128)(2,1)} %copy.3.yh, bf16[256,256]{1,0:T(8,128)(2,1)} %copy.4.yl, f32[4,32,64,128]{3,2,1,0:T(8,128)} %bitcast.8.in_ref), custom_call_target="tpu_custom_call" | custom-call | flops 2415919104 | bytes 8388608 | tf_op jit(solution)/shard_map/planes_in/pallas_call | solution.py:239
  259.1 32.8 %all-to-all-done.2 = f32[128,64,128]{2,1,0:T(8,128)} async-done(((f32[128,64,128]{2,1,0:T(8,128)}), f32[128,64,128]{2,1,0:T(8,128)}, u32[]{:S(2)}, u32[]{:S(2)}) %all-to-all-start.2) | async-done | bytes 4194336 | tf_op jit(solution)/shard_map/all_to_all | solution.py:26
  292.0 15.2 %planes_in.2 = f32[4,16,128,128]{3,2,1,0:T(8,128)} custom-call(bf16[128,128]{1,0:T(8,128)(2,1)} %get-tuple-element.25.xh, bf16[128,128]{1,0:T(8,128)(2,1)} %get-tuple-element.26.xl, bf16[256,256]{1,0:T(8,128)(2,1)} %copy.3.yh, bf16[256,256]{1,0:T(8,128)(2,1)} %copy.4.yl, f32[4,32,64,128]{3,2,1,0:T(8,128)} %bitcast.6.in_ref), custom_call_target="tpu_custom_call" | custom-call | flops 2415919104 | bytes 8388608 | tf_op jit(solution)/shard_map/planes_in/pallas_call | solution.py:239
  307.2 19.2 %columns.1 = (f32[64,128,128]{2,1,0:T(8,128)}, f32[64,128,128]{2,1,0:T(8,128)}) custom-call(bf16[2,128,128]{2,1,0:T(8,128)(2,1)} %get-tuple-element.20.zh, bf16[2,128,128]{2,1,0:T(8,128)(2,1)} %get-tuple-element.19.zl, f32[64,128,128]{2,1,0:T(8,128)} %bitcast.46, f32[64,128,128]{2,1,0:T(8,128)} %bitcast.45), custom_call_target="tpu_custom_call" | custom-call | flops 3221225472 | bytes 16777216 | tf_op jit(solution)/shard_map/columns/pallas_call | solution.py:296
  326.4 12.4 %planes_out.3 = f32[4,32,64,128]{3,2,1,0:T(8,128)} custom-call(bf16[128,128]{1,0:T(8,128)(2,1)} %get-tuple-element.25.xh, bf16[128,128]{1,0:T(8,128)(2,1)} %get-tuple-element.26.xl, bf16[256,256]{1,0:T(8,128)(2,1)} %get-tuple-element.18.yh, bf16[256,256]{1,0:T(8,128)(2,1)} %get-tuple-element.17.yl, f32[4,16,128,128]{3,2,1,0:T(8,128)} %bitcast.47), custom_call_target="tpu_custom_call" | custom-call | flops 2415919104 | bytes 8388608 | tf_op jit(solution)/shard_map/planes_out/pallas_call | solution.py:239
  338.8 6.0 %all-to-all-start.5 = ((f32[128,64,128]{2,1,0:T(8,128)}), f32[128,64,128]{2,1,0:T(8,128)}, u32[]{:S(2)}, u32[]{:S(2)}) async-start(f32[128,64,128]{2,1,0:T(8,128)} %bitcast.36), calls=%async_computation.5 | async-start | bytes 8388608 | tf_op jit(solution)/shard_map/all_to_all | solution.py:26
  344.8 12.5 %planes_out.2 = f32[4,32,64,128]{3,2,1,0:T(8,128)} custom-call(bf16[128,128]{1,0:T(8,128)(2,1)} %get-tuple-element.25.xh, bf16[128,128]{1,0:T(8,128)(2,1)} %get-tuple-element.26.xl, bf16[256,256]{1,0:T(8,128)(2,1)} %get-tuple-element.18.yh, bf16[256,256]{1,0:T(8,128)(2,1)} %get-tuple-element.17.yl, f32[4,16,128,128]{3,2,1,0:T(8,128)} %bitcast.44), custom_call_target="tpu_custom_call" | custom-call | flops 2415919104 | bytes 8388608 | tf_op jit(solution)/shard_map/planes_out/pallas_call | solution.py:239
  357.3 40.7 %all-to-all-done.5 = f32[128,64,128]{2,1,0:T(8,128)} async-done(((f32[128,64,128]{2,1,0:T(8,128)}), f32[128,64,128]{2,1,0:T(8,128)}, u32[]{:S(2)}, u32[]{:S(2)}) %all-to-all-start.5) | async-done | bytes 4194336 | tf_op jit(solution)/shard_map/all_to_all | solution.py:26
  398.0 59.4 %all_to_all.32 = f32[128,64,128]{2,1,0:T(8,128)} all-to-all(f32[128,64,128]{2,1,0:T(8,128)} %bitcast.37), channel_id=1, replica_groups=mesh['slab'=4,'wide'=32] {'slab','wide'}, dimensions={0} | all-to-all | bytes 8388608 | tf_op jit(solution)/shard_map/all_to_all | solution.py:26
  457.4 11.0 %pad_maximum_fusion = f32[128,32,4,128]{3,2,1,0:T(4,128)} fusion(f32[128,16,4,128]{3,2,1,0:T(4,128)} %bitcast.15, f32[128,16,4,128]{3,2,1,0:T(4,128)} %bitcast.35), kind=kLoop, calls=%fused_computation | loop fusion | flops 2097152 | bytes 16777216 | tf_op jit(solution)/shard_map/concatenate | solution.py:352
  (10 shorter events, 1.1 us)
Async XLA Ops:
  173.6 59.2 %all-to-all-start.3 = ((f32[128,64,128]{2,1,0:T(8,128)}), f32[128,64,128]{2,1,0:T(8,128)}, u32[]{:S(2)}, u32[]{:S(2)}) async-start(f32[128,64,128]{2,1,0:T(8,128)} %fit.3), calls=%async_computation.3 | async-start | bytes 8388608 | tf_op jit(solution)/shard_map/all_to_all | solution.py:26
  232.8 59.2 %all-to-all-start.2 = ((f32[128,64,128]{2,1,0:T(8,128)}), f32[128,64,128]{2,1,0:T(8,128)}, u32[]{:S(2)}, u32[]{:S(2)}) async-start(f32[128,64,128]{2,1,0:T(8,128)} %fit.2), calls=%async_computation.2 | async-start | bytes 8388608 | tf_op jit(solution)/shard_map/all_to_all | solution.py:26
  338.8 59.2 %all-to-all-start.5 = ((f32[128,64,128]{2,1,0:T(8,128)}), f32[128,64,128]{2,1,0:T(8,128)}, u32[]{:S(2)}, u32[]{:S(2)}) async-start(f32[128,64,128]{2,1,0:T(8,128)} %bitcast.36), calls=%async_computation.5 | async-start | bytes 8388608 | tf_op jit(solution)/shard_map/all_to_all | solution.py:26

commit v3 on v2

--- a/solution.py
+++ b/solution.py
@@ -11,7 +11,7 @@
 AXES = ("slab", "wide")
 HI = lax.Precision.HIGHEST
 BLK = 128
-CHUNKS = 2
+PARTS = (8, 16, 8)
 SLOTS = 8
 
 
@@ -124,10 +124,11 @@
             groups[i] = base - col * scaled
     return jnp.concatenate(groups, axis=0)
 
-def coeff_kernel(s_ref, out_ref, g_ref, p_ref, l_ref):
+def coeff_kernel(s_ref, ch_ref, cl_ref, sh_ref, sl_ref, out_ref, g_ref, p_ref, l_ref):
     n = s_ref.shape[0]
     nb = n // BLK
     rows = s_ref[...]
+    sh_ref[...], sl_ref[...] = halves(rows)
     corr = lax.dot_general(rows, rows, (((1,), (1,)), ((), ())), precision=HI, preferred_element_type=jnp.float32)
     gram = corr * corr
     r = lax.broadcasted_iota(jnp.int32, (n, n), 0)
@@ -158,29 +159,38 @@
         lo = b * BLK
         part = lax.dot_general(out_ref[:, 0:lo], p_ref[lo : lo + BLK, 0:lo], (((1,), (1,)), ((), ())), precision=HI, preferred_element_type=jnp.float32)
         out_ref[:, lo : lo + BLK] = -jnp.dot(part, l_ref[lo : lo + BLK, :], precision=HI, preferred_element_type=jnp.float32)
+    ch_ref[...], cl_ref[...] = halves(out_ref[...])
+
 
 def coefficients(rows):
-    n = rows.shape[0]
-    return pl.pallas_call(
+    n, width = rows.shape
+    coeff = jax.ShapeDtypeStruct((BLK, n), jnp.bfloat16)
+    sample = jax.ShapeDtypeStruct((n, width), jnp.bfloat16)
+    ch, cl, sh, sl = pl.pallas_call(
         coeff_kernel,
-        out_shape=jax.ShapeDtypeStruct((BLK, n), jnp.float32),
-        scratch_shapes=[pltpu.VMEM((n, n), jnp.float32), pltpu.VMEM((n, n), jnp.float32), pltpu.VMEM((n, BLK), jnp.float32)],
+        out_shape=[coeff, coeff, sample, sample],
+        scratch_shapes=[
+            pltpu.VMEM((BLK, n), jnp.float32),
+            pltpu.VMEM((n, n), jnp.float32),
+            pltpu.VMEM((n, n), jnp.float32),
+            pltpu.VMEM((n, BLK), jnp.float32),
+        ],
         name="coefficients",
     )(rows)
+    return (ch, cl), (sh, sl)
 
 
 def fit_kernel(sh, sl, ch, cl, orb, out_ref, bh, bl):
     lines = orb.shape[1]
+    turned = jnp.transpose(orb[...], (1, 0, 2))
     for r in range(lines):
-        top, low = halves(orb[:, r, :])
+        top, low = halves(turned[r])
         bh[:, r * BLK : (r + 1) * BLK] = top
         bl[:, r * BLK : (r + 1) * BLK] = low
-    for r in range(0, lines, 4):
-        cut = slice(r * BLK, (r + 4) * BLK)
-        pairs = mul3((sh[...], sl[...]), (bh[:, cut], bl[:, cut]))
-        piece = mul3((ch[...], cl[...]), halves(pairs * pairs))
-        for k in range(4):
-            out_ref[:, r + k, :] = piece[:, k * BLK : (k + 1) * BLK]
+    pairs = mul3((sh[...], sl[...]), (bh[...], bl[...]))
+    piece = mul3((ch[...], cl[...]), halves(pairs * pairs))
+    piece = jnp.stack([piece[:, r * BLK : (r + 1) * BLK] for r in range(lines)], axis=0)
+    out_ref[...] = jnp.transpose(piece, (1, 0, 2))
 
 
 def fit(sampled, coeffs, orbitals, first, count, lines=8):
@@ -213,33 +223,38 @@
 
 
 def planes_in_kernel(xh, xl, yh, yl, in_ref, out_ref):
-    for pair in range(in_ref.shape[2] // 8):
-        tile = in_ref[0, :, 8 * pair : 8 * pair + 8, :].reshape(2 * BLK, BLK)
-        along = mul3(halves(tile), (xh[...], xl[...]))
-        both = mul3((yh[...], yl[...]), halves(along))
-        out_ref[0, 2 * pair] = both[:BLK]
-        out_ref[0, 2 * pair + 1] = both[BLK:]
+    pairs = in_ref.shape[2] // 8
+    for p in range(0, pairs, 4):
+        tall = [in_ref[0, :, 8 * (p + g) : 8 * (p + g) + 8, :].reshape(2 * BLK, BLK) for g in range(4)]
+        along = mul3(halves(jnp.concatenate(tall, axis=0)), (xh[...], xl[...]))
+        wide = [along[2 * BLK * g : 2 * BLK * (g + 1)] for g in range(4)]
+        both = mul3((yh[...], yl[...]), halves(jnp.concatenate(wide, axis=1)))
+        for g in range(4):
+            out_ref[0, 2 * (p + g)] = both[:BLK, BLK * g : BLK * (g + 1)]
+            out_ref[0, 2 * (p + g) + 1] = both[BLK:, BLK * g : BLK * (g + 1)]
 
 
 def planes_out_kernel(xh, xl, yh, yl, in_ref, out_ref):
-    for pair in range(in_ref.shape[1] // 2):
-        tile = jnp.concatenate([in_ref[0, 2 * pair], in_ref[0, 2 * pair + 1]], axis=0)
-        both = mul3((yh[...], yl[...]), halves(tile))
-        along = mul3(halves(both), (xh[...], xl[...]))
-        out_ref[0, :, 8 * pair : 8 * pair + 8, :] = along.reshape(32, 8, BLK)
-
-
-def planes(kernel, xtab, ytab, values, out_shape, name, step=8):
-    slabs, depth = (values.shape[0], values.shape[2] // 4) if name == "planes_in" else values.shape[:2]
-    cellwise = pl.BlockSpec((1, 32, 4 * step, BLK), lambda s, i: (s, 0, i, 0))
-    planewise = pl.BlockSpec((1, step, BLK, BLK), lambda s, i: (s, i, 0, 0))
-    small = pl.BlockSpec((BLK, BLK), lambda s, i: (0, 0))
-    large = pl.BlockSpec((2 * BLK, 2 * BLK), lambda s, i: (0, 0))
+    pairs = in_ref.shape[1] // 2
+    wide = [in_ref[0, 2 * g : 2 * g + 2].reshape(2 * BLK, BLK) for g in range(pairs)]
+    both = mul3((yh[...], yl[...]), halves(jnp.concatenate(wide, axis=1)))
+    tall = [both[:, BLK * g : BLK * (g + 1)] for g in range(pairs)]
+    along = mul3(halves(jnp.concatenate(tall, axis=0)), (xh[...], xl[...]))
+    for g in range(pairs):
+        out_ref[0, :, 8 * g : 8 * g + 8, :] = along[2 * BLK * g : 2 * BLK * (g + 1)].reshape(32, 8, BLK)
+
+
+def planes(kernel, xtab, ytab, values, out_shape, name):
     inward = name == "planes_in"
+    slabs, depth = (values.shape[0], values.shape[2] // 4) if inward else values.shape[:2]
+    cellwise = pl.BlockSpec((1, 32, 4 * depth, BLK), lambda s: (s, 0, 0, 0))
+    planewise = pl.BlockSpec((1, depth, BLK, BLK), lambda s: (s, 0, 0, 0))
+    small = pl.BlockSpec((BLK, BLK), lambda s: (0, 0))
+    large = pl.BlockSpec((2 * BLK, 2 * BLK), lambda s: (0, 0))
     return pl.pallas_call(
         kernel,
         out_shape=jax.ShapeDtypeStruct(out_shape, jnp.float32),
-        grid=(slabs, depth // step),
+        grid=(slabs,),
         in_specs=[small, small, large, large, cellwise if inward else planewise],
         out_specs=planewise if inward else cellwise,
         cost_estimate=pl.CostEstimate(
@@ -263,47 +278,72 @@
     zsq = square(lax.broadcasted_iota(jnp.int32, (BLK, BLK), 0))
     xsq = square(lax.broadcasted_iota(jnp.int32, (BLK, BLK), 1))
     flat = zsq + xsq
-    part = BLK // count
-    for j in range(0, lines, 2):
-        tile = jnp.concatenate(
-            [
-                jnp.concatenate([ref[:, j, :] for ref in ins], axis=0),
-                jnp.concatenate([ref[:, j + 1, :] for ref in ins], axis=0),
-            ],
-            axis=1,
-        )
-        spec = mul3((zh[0], zl[0]), halves(tile))
-        weights = []
-        for k in range(2):
-            index = base + j + k
-            total = flat + square(jnp.full((BLK, BLK), index, jnp.int32))
-            safe = jnp.where(total > 0, total, 1.0)
-            scale = 4.0 * math.pi / float(length**3)
-            weights.append(jnp.where(total > 0, scale / safe, 0.0))
-        spec = spec * jnp.concatenate(weights, axis=1)
-        back = mul3((zh[1], zl[1]), halves(spec))
-        for c, ref in enumerate(outs):
-            for k in range(2):
-                ref[:, j + k, :] = back[c * part : (c + 1) * part, k * BLK : (k + 1) * BLK]
+    tile = jnp.concatenate([jnp.transpose(ref[...], (1, 0, 2)) for ref in ins], axis=1)
+    spec = mul3((zh[0], zl[0]), halves(jnp.concatenate([tile[j] for j in range(lines)], axis=1)))
+    scale = 4.0 * math.pi / float(length**3)
+    weights = []
+    for j in range(lines):
+        total = flat + square(jnp.full((BLK, BLK), base + j, jnp.int32))
+        safe = jnp.where(total > 0, total, 1.0)
+        weights.append(jnp.where(total > 0, scale / safe, 0.0))
+    spec = spec * jnp.concatenate(weights, axis=1)
+    back = mul3((zh[1], zl[1]), halves(spec))
+    back = jnp.stack([back[:, j * BLK : (j + 1) * BLK] for j in range(lines)], axis=0)
+    start = 0
+    for ref in outs:
+        part = ref.shape[0]
+        ref[...] = jnp.transpose(back[:, start : start + part], (1, 0, 2))
+        start += part
 
 
 def columns(ztab, values, lines=8):
     count = len(values)
-    part = BLK // count
-    spec = pl.BlockSpec((part, lines, BLK), lambda i: (0, i, 0))
+    specs = [pl.BlockSpec((v.shape[0], lines, BLK), lambda i: (0, i, 0)) for v in values]
     table = pl.BlockSpec((2, BLK, BLK), lambda i: (0, 0, 0))
     size = BLK**3
     return pl.pallas_call(
         functools.partial(columns_kernel, count),
-        out_shape=[jax.ShapeDtypeStruct((part, BLK, BLK), jnp.float32)] * count,
+        out_shape=[jax.ShapeDtypeStruct(v.shape, jnp.float32) for v in values],
         grid=(BLK // lines,),
-        in_specs=[table, table] + [spec] * count,
-        out_specs=[spec] * count,
+        in_specs=[table, table] + specs,
+        out_specs=specs,
         cost_estimate=pl.CostEstimate(
             flops=12 * size * BLK, transcendentals=size, bytes_accessed=8 * size
         ),
         name="columns",
     )(*ztab, *values)
+
+
+def join_kernel(first, src, *refs):
+    out, sems = refs[-2], refs[-1]
+    quarter = src.shape[0] // 4
+    copies = [
+        pltpu.make_async_copy(
+            src.at[pl.ds(k * quarter, quarter)],
+            out.at[pl.ds(k * quarter, quarter), pl.ds(first, src.shape[1])],
+            sems.at[k],
+        )
+        for k in range(4)
+    ]
+    for copy in copies:
+        copy.start()
+    for copy in copies:
+        copy.wait()
+
+
+def join(piece, whole, first, shape):
+    anywhere = pl.BlockSpec(memory_space=pl.ANY)
+    args = (piece,) if whole is None else (piece, whole)
+    return pl.pallas_call(
+        functools.partial(join_kernel, first),
+        out_shape=jax.ShapeDtypeStruct(shape, jnp.float32),
+        in_specs=[whole_spec()] + [anywhere] * (len(args) - 1),
+        out_specs=anywhere,
+        input_output_aliases={} if whole is None else {1: 0},
+        scratch_shapes=[pltpu.SemaphoreType.DMA((4,))],
+        cost_estimate=pl.CostEstimate(flops=0, transcendentals=0, bytes_accessed=8 * piece.size),
+        name="join",
+    )(*args)
 
 
 def per_device(orbitals, points):
@@ -323,33 +363,36 @@
     mine = exchange(picked.reshape(devices, npoint // devices, norbit)).sum(0)
     sampled_rows = exchange(jnp.broadcast_to(mine[None], (devices,) + mine.shape))
     sampled_rows = sampled_rows.reshape(npoint, norbit)
-    coeffs = split(coefficients(sampled_rows))
-    sampled = split(sampled_rows)
-
+    coeffs, sampled = coefficients(sampled_rows)
     table = hartley(grid)
     xtab = split(table)
-    part = depth // CHUNKS
     lines = table.reshape(grid, wides, 1, rows)
     eye = jnp.eye(2, dtype=jnp.float32)
     ysplit = (eye[:, None, None, :, None] * lines[None]).reshape(2 * grid, wides * 2 * rows)
-    ztable = table.reshape(grid, slabs, CHUNKS, part).transpose(0, 2, 1, 3).reshape(grid, grid)
+    starts = [sum(PARTS[:c]) for c in range(len(PARTS))]
+    zrows = table.reshape(grid, slabs, depth)
+    ztable = jnp.concatenate(
+        [zrows[:, :, lo : lo + part].reshape(grid, slabs * part) for lo, part in zip(starts, PARTS)], axis=1
+    )
     yin, yout = split(ysplit), split(ysplit.T)
     ztab = split(jnp.stack([ztable, ztable.T]))
 
     flat = orbitals.reshape(norbit, depth * rows, grid)
     spectra = []
-    for c in range(CHUNKS):
-        piece = fit(sampled, coeffs, flat, c * part * rows, part * rows)
+    for lo, part in zip(starts, PARTS):
+        piece = fit(sampled, coeffs, flat, lo * rows, part * rows)
+        piece, flat = lax.optimization_barrier((piece, flat))
         whole = exchange(piece).reshape(slabs, wides, part * rows, grid)
         spec = planes(planes_in_kernel, xtab, yin, whole, (slabs, part, grid, grid), "planes_in")
         spectra.append(spec.reshape(slabs * part, grid, grid))
     spectra = columns(ztab, spectra)
-    out = []
-    for c in range(CHUNKS):
-        spec = spectra[c].reshape(slabs, part, grid, grid)
+    out = None
+    for spec, lo, part in zip(spectra, starts, PARTS):
+        spec = spec.reshape(slabs, part, grid, grid)
         back = planes(planes_out_kernel, xtab, yout, spec, (slabs, wides, part * rows, grid), "planes_out")
-        out.append(exchange(back.reshape(devices, part * rows, grid)).reshape(devices, part, rows, grid))
-    return jnp.concatenate(out, axis=1)
+        piece = exchange(back.reshape(devices, part * rows, grid)).reshape(devices, part, rows, grid)
+        out = join(piece, out, lo, (devices, depth, rows, grid))
+    return out
 
 
 def solution(mesh):

time: 469 us -> 440 us (0.938)
  Pallas kernels: 239 us -> 190 us
  waiting for transfers between devices: 88.8 us -> 136 us
  blocking collectives: 97.9 us -> 73.8 us
  other arithmetic: 20.4 us -> 5.67 us
  starting transfers between devices: 17.9 us -> 25.8 us
    all_to_all x3 -> x5, waiting for transfers between devices: 88.8 us -> 136 us  [exchange(): return lax.all_to_all(blocks, AXES, split_axis=0, concat_axis=0, tiled=True)]
    pallas_call x2 -> x3, Pallas kernels: 76 us -> 33.7 us  [fit(): pl.pallas_call(fit_kernel, out_shape=jax.ShapeDtypeStruct((vectors, count...]
    all_to_all x3, blocking collectives: 97.9 us -> 73.8 us  [exchange(): return lax.all_to_all(blocks, AXES, split_axis=0, concat_axis=0, tiled=True)]
    pallas_call x4 -> x6, Pallas kernels: 55.3 us -> 38.8 us  [planes(): pl.pallas_call(kernel, out_shape=jax.ShapeDtypeStruct(out_shape, jnp.floa...]
    concatenate x1 -> x0, other arithmetic: 11 us -> none  [per_device(): return jnp.concatenate(out, axis=1)]
    pallas_call x1 -> x4, Pallas kernels: 77.7 us -> 87.9 us  [the longest x1 77.8 us: coefficients(): pl.pallas_call(coeff_kernel, out_shape=[coeff, coeff, sample, sample], sc...]
    all_to_all x3 -> x5, starting transfers between devices: 17.9 us -> 25.8 us  [exchange(): return lax.all_to_all(blocks, AXES, split_axis=0, concat_axis=0, tiled=True)]
  transfers between devices with their start and end apart: 3 -> 5, of which waited for: 3 -> 5; matrix products, arithmetic and copies ran while one was open for 1% -> 1% of each run, Pallas kernels for 14% -> 13%
where the time goes in v3:
time: 440 us; the launch traced here: 438 us
  Pallas kernels  190 us (43%)
  waiting for transfers between devices  136 us (31%)
  blocking collectives  73.8 us (17%)
  starting transfers between devices  25.8 us (6%)
  local copies, waits for them, and re-layouts  6.57 us (1%)
  other arithmetic  5.67 us (1%)
    all_to_all x5, waiting for transfers between devices, exchange(): return lax.all_to_all(blocks, AXES, split_axis=0, concat_axis=0, tiled=True)  136 us
    pallas_call x1, Pallas kernels, coefficients(): pl.pallas_call(coeff_kernel, out_shape=[coeff, coeff, sample, sample], sc...  77.8 us
    all_to_all x3, blocking collectives, exchange(): return lax.all_to_all(blocks, AXES, split_axis=0, concat_axis=0, tiled=True)  73.8 us
    pallas_call x6, Pallas kernels, planes(): pl.pallas_call(kernel, out_shape=jax.ShapeDtypeStruct(out_shape, jnp.floa...  38.8 us
    pallas_call x3, Pallas kernels, fit(): pl.pallas_call(fit_kernel, out_shape=jax.ShapeDtypeStruct((vectors, count...  33.7 us
    all_to_all x5, starting transfers between devices, exchange(): return lax.all_to_all(blocks, AXES, split_axis=0, concat_axis=0, tiled=True)  25.8 us
    pallas_call x1, Pallas kernels, columns(): pl.pallas_call(functools.partial(columns_kernel, count), out_shape=[jax.S...  17.8 us
    pallas_call x1, Pallas kernels, pick(): pl.pallas_call(pick_kernel, out_shape=jax.ShapeDtypeStruct((npoint, norbi...  11.8 us
  transfers between devices with their start and end apart: 5, of which 5 were waited for; matrix products, arithmetic and copies ran while one was open for 1% of the time, Pallas kernels for 13%

profile of v3, /device:TPU:0, one launch (start us, length us, event | category | flops | bytes accessed | tf_op | source)
XLA Modules:
  0.0 437.8 jit_solution(15977645575417394982)
XLA Ops:
  2.0 11.8 %pick.1 = f32[512,256]{1,0:T(8,128)} custom-call(s32[4,512]{1,0:T(4,128)} %pad_add_fusion.info, f32[256,32,4,128]{3,2,1,0:T(4,128)} %orb.1), custom_call_target="tpu_custom_call" | custom-call | tf_op jit(solution)/shard_map/pick/pallas_call | solution.py:90
  13.9 1.2 reshape.126
  15.1 19.8 %all_to_all.40 = f32[128,4,256]{2,1,0:T(4,128)S(1)} all-to-all(f32[128,4,256]{2,1,0:T(4,128)S(1)} %reshape.126), channel_id=1, replica_groups=mesh['slab'=4,'wide'=32] {'slab','wide'}, dimensions={0} | all-to-all | bytes 1048576 | tf_op jit(solution)/shard_map/all_to_all | solution.py:26
  35.1 18.1 %all_to_all.41 = f32[128,4,256]{2,1,0:T(4,128)S(1)} all-to-all(f32[128,4,256]{2,1,0:T(4,128)S(1)} %broadcast_in_dim.2), channel_id=1, replica_groups=mesh['slab'=4,'wide'=32] {'slab','wide'}, dimensions={0} | all-to-all | bytes 1048576 | tf_op jit(solution)/shard_map/all_to_all | solution.py:26
  53.1 1.0 reshape.127.s_ref
  54.1 77.8 %coefficients.1 = (bf16[128,512]{1,0:T(8,128)(2,1)}, bf16[128,512]{1,0:T(8,128)(2,1)}, bf16[512,256]{1,0:T(8,128)(2,1)}, bf16[512,256]{1,0:T(8,128)(2,1)}) custom-call(f32[512,256]{1,0:T(8,128)} %reshape.127.s_ref), custom_call_target="tpu_custom_call" | custom-call | tf_op jit(solution)/shard_map/coefficients/pallas_call | solution.py:169
  131.9 9.0 %fit.3 = f32[128,32,128]{2,1,0:T(8,128)} custom-call(bf16[512,256]{1,0:T(8,128)(2,1)} %get-tuple-element.17.sh, bf16[512,256]{1,0:T(8,128)(2,1)} %get-tuple-element.18.sl, bf16[128,512]{1,0:T(8,128)(2,1)} %get-tuple-element.19.ch, bf16[128,512]{1,0:T(8,128)(2,1)} %get-tuple-element.20.cl, f32[256,128,128]{2,1,0:T(8,128)} %bitcast.49), custom_call_target="tpu_custom_call" | custom-call | flops 4831838208 | bytes 6291456 | tf_op jit(solution)/shard_map/fit/pallas_call | solution.py:200
  140.9 4.8 %all-to-all-start.2 = ((f32[128,32,128]{2,1,0:T(8,128)}), f32[128,32,128]{2,1,0:T(8,128)S(1)}, u32[]{:S(2)}, u32[]{:S(2)}) async-start(f32[128,32,128]{2,1,0:T(8,128)} %fit.3), calls=%async_computation.2 | async-start | bytes 4194304 | tf_op jit(solution)/shard_map/all_to_all | solution.py:26
  145.7 15.7 %fit.4 = f32[128,64,128]{2,1,0:T(8,128)} custom-call(bf16[512,256]{1,0:T(8,128)(2,1)} %get-tuple-element.17.sh, bf16[512,256]{1,0:T(8,128)(2,1)} %get-tuple-element.18.sl, bf16[128,512]{1,0:T(8,128)(2,1)} %get-tuple-element.19.ch, bf16[128,512]{1,0:T(8,128)(2,1)} %get-tuple-element.20.cl, f32[256,128,128]{2,1,0:T(8,128)} %bitcast.50), custom_call_target="tpu_custom_call" | custom-call | flops 9663676416 | bytes 12582912 | tf_op jit(solution)/shard_map/fit/pallas_call | solution.py:200
  161.4 9.0 %fit.5 = f32[128,32,128]{2,1,0:T(8,128)} custom-call(bf16[512,256]{1,0:T(8,128)(2,1)} %get-tuple-element.17.sh, bf16[512,256]{1,0:T(8,128)(2,1)} %get-tuple-element.18.sl, bf16[128,512]{1,0:T(8,128)(2,1)} %get-tuple-element.19.ch, bf16[128,512]{1,0:T(8,128)(2,1)} %get-tuple-element.20.cl, f32[256,128,128]{2,1,0:T(8,128)} %bitcast.51), custom_call_target="tpu_custom_call" | custom-call | flops 4831838208 | bytes 6291456 | tf_op jit(solution)/shard_map/fit/pallas_call | solution.py:200
  170.4 5.5 %all-to-all-done.2 = f32[128,32,128]{2,1,0:T(8,128)S(1)} async-done(((f32[128,32,128]{2,1,0:T(8,128)}), f32[128,32,128]{2,1,0:T(8,128)S(1)}, u32[]{:S(2)}, u32[]{:S(2)}) %all-to-all-start.2) | async-done | bytes 2097184 | tf_op jit(solution)/shard_map/all_to_all | solution.py:26
  176.0 36.0 %all_to_all.42 = f32[128,32,128]{2,1,0:T(8,128)} all-to-all(f32[128,32,128]{2,1,0:T(8,128)} %fit.5), channel_id=1, replica_groups=mesh['slab'=4,'wide'=32] {'slab','wide'}, dimensions={0} | all-to-all | bytes 4194304 | tf_op jit(solution)/shard_map/all_to_all | solution.py:26
  212.0 5.8 %all-to-all-start.3 = ((f32[128,64,128]{2,1,0:T(8,128)}), f32[128,64,128]{2,1,0:T(8,128)}, u32[]{:S(2)}, u32[]{:S(2)}) async-start(f32[128,64,128]{2,1,0:T(8,128)} %fit.4), calls=%async_computation.3 | async-start | bytes 8388608 | tf_op jit(solution)/shard_map/all_to_all | solution.py:26
  223.0 6.3 %planes_in.3 = f32[4,8,128,128]{3,2,1,0:T(8,128)} custom-call(bf16[128,128]{1,0:T(8,128)(2,1)} %get-tuple-element.43.xh, bf16[128,128]{1,0:T(8,128)(2,1)} %get-tuple-element.44.xl, bf16[256,256]{1,0:T(8,128)(2,1)} %copy.6.yh, bf16[256,256]{1,0:T(8,128)(2,1)} %copy.7.yl, f32[4,32,32,128]{3,2,1,0:T(8,128)} %bitcast.54), custom_call_target="tpu_custom_call" | custom-call | flops 1207959552 | bytes 4194304 | tf_op jit(solution)/shard_map/planes_in/pallas_call | solution.py:254
  229.3 6.3 %planes_in.5 = f32[4,8,128,128]{3,2,1,0:T(8,128)} custom-call(bf16[128,128]{1,0:T(8,128)(2,1)} %get-tuple-element.43.xh, bf16[128,128]{1,0:T(8,128)(2,1)} %get-tuple-element.44.xl, bf16[256,256]{1,0:T(8,128)(2,1)} %copy.6.yh, bf16[256,256]{1,0:T(8,128)(2,1)} %copy.7.yl, f32[4,32,32,128]{3,2,1,0:T(8,128)} %bitcast.55), custom_call_target="tpu_custom_call" | custom-call | flops 1207959552 | bytes 4194304 | tf_op jit(solution)/shard_map/planes_in/pallas_call | solution.py:254
  235.6 35.6 %all-to-all-done.3 = f32[128,64,128]{2,1,0:T(8,128)} async-done(((f32[128,64,128]{2,1,0:T(8,128)}), f32[128,64,128]{2,1,0:T(8,128)}, u32[]{:S(2)}, u32[]{:S(2)}) %all-to-all-start.3) | async-done | bytes 4194336 | tf_op jit(solution)/shard_map/all_to_all | solution.py:26
  271.2 8.2 %planes_in.4 = f32[4,16,128,128]{3,2,1,0:T(8,128)} custom-call(bf16[128,128]{1,0:T(8,128)(2,1)} %get-tuple-element.43.xh, bf16[128,128]{1,0:T(8,128)(2,1)} %get-tuple-element.44.xl, bf16[256,256]{1,0:T(8,128)(2,1)} %copy.6.yh, bf16[256,256]{1,0:T(8,128)(2,1)} %copy.7.yl, f32[4,32,64,128]{3,2,1,0:T(8,128)} %bitcast.14.in_ref), custom_call_target="tpu_custom_call" | custom-call | flops 2415919104 | bytes 8388608 | tf_op jit(solution)/shard_map/planes_in/pallas_call | solution.py:254
  279.3 17.8 %columns.1 = (f32[32,128,128]{2,1,0:T(8,128)}, f32[64,128,128]{2,1,0:T(8,128)}, f32[32,128,128]{2,1,0:T(8,128)}) custom-call(bf16[2,128,128]{2,1,0:T(8,128)(2,1)} %get-tuple-element.36.zh, bf16[2,128,128]{2,1,0:T(8,128)(2,1)} %get-tuple-element.35.zl, f32[32,128,128]{2,1,0:T(8,128)} %bitcast.62, f32[64,128,128]{2,1,0:T(8,128)} %bitcast.71, ...), custom_call_target="tpu_custom_call" | custom-call | flops 3221225472 | bytes 16777216 | tf_op jit(solution)/shard_map/columns/pallas_call | solution.py:304
  297.1 5.5 %planes_out.5 = f32[4,32,32,128]{3,2,1,0:T(8,128)} custom-call(bf16[128,128]{1,0:T(8,128)(2,1)} %get-tuple-element.43.xh, bf16[128,128]{1,0:T(8,128)(2,1)} %get-tuple-element.44.xl, bf16[256,256]{1,0:T(8,128)(2,1)} %get-tuple-element.34.yh, bf16[256,256]{1,0:T(8,128)(2,1)} %get-tuple-element.33.yl, f32[4,8,128,128]{3,2,1,0:T(8,128)} %bitcast.64), custom_call_target="tpu_custom_call" | custom-call | flops 1207959552 | bytes 4194304 | tf_op jit(solution)/shard_map/planes_out/pallas_call | solution.py:254
  302.6 4.6 %all-to-all-start.7 = ((f32[128,32,128]{2,1,0:T(8,128)}), f32[128,32,128]{2,1,0:T(8,128)S(1)}, u32[]{:S(2)}, u32[]{:S(2)}) async-start(f32[128,32,128]{2,1,0:T(8,128)} %bitcast.57), calls=%async_computation.7 | async-start | bytes 4194304 | tf_op jit(solution)/shard_map/all_to_all | solution.py:26
  307.3 7.1 %planes_out.4 = f32[4,32,64,128]{3,2,1,0:T(8,128)} custom-call(bf16[128,128]{1,0:T(8,128)(2,1)} %get-tuple-element.43.xh, bf16[128,128]{1,0:T(8,128)(2,1)} %get-tuple-element.44.xl, bf16[256,256]{1,0:T(8,128)(2,1)} %get-tuple-element.34.yh, bf16[256,256]{1,0:T(8,128)(2,1)} %get-tuple-element.33.yl, f32[4,16,128,128]{3,2,1,0:T(8,128)} %bitcast.70), custom_call_target="tpu_custom_call" | custom-call | flops 2415919104 | bytes 8388608 | tf_op jit(solution)/shard_map/planes_out/pallas_call | solution.py:254
  314.4 23.3 %all-to-all-done.7 = f32[128,32,128]{2,1,0:T(8,128)S(1)} async-done(((f32[128,32,128]{2,1,0:T(8,128)}), f32[128,32,128]{2,1,0:T(8,128)S(1)}, u32[]{:S(2)}, u32[]{:S(2)}) %all-to-all-start.7) | async-done | bytes 2097184 | tf_op jit(solution)/shard_map/all_to_all | solution.py:26
  337.7 1.4 copy-done
  339.1 5.8 %all-to-all-start.6 = ((f32[128,64,128]{2,1,0:T(8,128)}), f32[128,64,128]{2,1,0:T(8,128)}, u32[]{:S(2)}, u32[]{:S(2)}) async-start(f32[128,64,128]{2,1,0:T(8,128)} %bitcast.58), calls=%async_computation.6 | async-start | bytes 8388608 | tf_op jit(solution)/shard_map/all_to_all | solution.py:26
  344.9 5.5 %planes_out.3 = f32[4,32,32,128]{3,2,1,0:T(8,128)} custom-call(bf16[128,128]{1,0:T(8,128)(2,1)} %get-tuple-element.43.xh, bf16[128,128]{1,0:T(8,128)(2,1)} %get-tuple-element.44.xl, bf16[256,256]{1,0:T(8,128)(2,1)} %get-tuple-element.34.yh, bf16[256,256]{1,0:T(8,128)(2,1)} %get-tuple-element.33.yl, f32[4,8,128,128]{3,2,1,0:T(8,128)} %bitcast.61), custom_call_target="tpu_custom_call" | custom-call | flops 1207959552 | bytes 4194304 | tf_op jit(solution)/shard_map/planes_out/pallas_call | solution.py:254
  350.4 47.8 %all-to-all-done.6 = f32[128,64,128]{2,1,0:T(8,128)} async-done(((f32[128,64,128]{2,1,0:T(8,128)}), f32[128,64,128]{2,1,0:T(8,128)}, u32[]{:S(2)}, u32[]{:S(2)}) %all-to-all-start.6) | async-done | bytes 4194336 | tf_op jit(solution)/shard_map/all_to_all | solution.py:26
  398.3 4.6 %all-to-all-start.5 = ((f32[128,32,128]{2,1,0:T(8,128)}), f32[128,32,128]{2,1,0:T(8,128)S(1)}, u32[]{:S(2)}, u32[]{:S(2)}) async-start(f32[128,32,128]{2,1,0:T(8,128)} %bitcast.56), calls=%async_computation.5 | async-start | bytes 4194304 | tf_op jit(solution)/shard_map/all_to_all | solution.py:26
  402.9 2.9 join.3.refs_0_
  405.9 4.2 join.4.refs_0_
  410.1 23.2 %all-to-all-done.5 = f32[128,32,128]{2,1,0:T(8,128)S(1)} async-done(((f32[128,32,128]{2,1,0:T(8,128)}), f32[128,32,128]{2,1,0:T(8,128)S(1)}, u32[]{:S(2)}, u32[]{:S(2)}) %all-to-all-start.5) | async-done | bytes 2097184 | tf_op jit(solution)/shard_map/all_to_all | solution.py:26
  433.3 1.3 copy-done.1
  434.7 2.9 join.5
  (26 shorter events, 7.4 us)
Async XLA Ops:
  140.9 35.1 %all-to-all-start.2 = ((f32[128,32,128]{2,1,0:T(8,128)}), f32[128,32,128]{2,1,0:T(8,128)S(1)}, u32[]{:S(2)}, u32[]{:S(2)}) async-start(f32[128,32,128]{2,1,0:T(8,128)} %fit.3), calls=%async_computation.2 | async-start | bytes 4194304 | tf_op jit(solution)/shard_map/all_to_all | solution.py:26
  175.9 36.0 %copy-start.2 = (f32[128,32,128]{2,1,0:T(8,128)}, f32[128,32,128]{2,1,0:T(8,128)S(1)}, u32[]{:S(2)}) copy-start(f32[128,32,128]{2,1,0:T(8,128)S(1)} %all-to-all-done.2) | copy-start | bytes 6291460
  212.0 59.2 %all-to-all-start.3 = ((f32[128,64,128]{2,1,0:T(8,128)}), f32[128,64,128]{2,1,0:T(8,128)}, u32[]{:S(2)}, u32[]{:S(2)}) async-start(f32[128,64,128]{2,1,0:T(8,128)} %fit.4), calls=%async_computation.3 | async-start | bytes 8388608 | tf_op jit(solution)/shard_map/all_to_all | solution.py:26
  302.6 35.1 %all-to-all-start.7 = ((f32[128,32,128]{2,1,0:T(8,128)}), f32[128,32,128]{2,1,0:T(8,128)S(1)}, u32[]{:S(2)}, u32[]{:S(2)}) async-start(f32[128,32,128]{2,1,0:T(8,128)} %bitcast.57), calls=%async_computation.7 | async-start | bytes 4194304 | tf_op jit(solution)/shard_map/all_to_all | solution.py:26
  337.7 1.4 copy-start
  339.1 59.2 %all-to-all-start.6 = ((f32[128,64,128]{2,1,0:T(8,128)}), f32[128,64,128]{2,1,0:T(8,128)}, u32[]{:S(2)}, u32[]{:S(2)}) async-start(f32[128,64,128]{2,1,0:T(8,128)} %bitcast.58), calls=%async_computation.6 | async-start | bytes 8388608 | tf_op jit(solution)/shard_map/all_to_all | solution.py:26
  398.3 35.1 %all-to-all-start.5 = ((f32[128,32,128]{2,1,0:T(8,128)}), f32[128,32,128]{2,1,0:T(8,128)S(1)}, u32[]{:S(2)}, u32[]{:S(2)}) async-start(f32[128,32,128]{2,1,0:T(8,128)} %bitcast.56), calls=%async_computation.5 | async-start | bytes 4194304 | tf_op jit(solution)/shard_map/all_to_all | solution.py:26
  433.3 1.3 copy-start.1

commit v4 on v3

--- a/solution.py
+++ b/solution.py
@@ -11,8 +11,9 @@
 AXES = ("slab", "wide")
 HI = lax.Precision.HIGHEST
 BLK = 128
-PARTS = (8, 16, 8)
+PARTS = (16, 16)
 SLOTS = 8
+PANEL = 16
 
 
 def hartley(length):
@@ -41,6 +42,14 @@
         return jnp.dot(a, b, preferred_element_type=jnp.float32)
 
     return one(left[0], right[0]) + (one(left[1], right[0]) + one(left[0], right[1]))
+
+
+def left3(high, low, value):
+    top = jnp.concatenate([high, high], axis=1)
+    bottom = jnp.concatenate([low, jnp.zeros_like(low)], axis=1)
+    table = jnp.concatenate([top, bottom], axis=0)
+    both = jnp.dot(table, jnp.concatenate(halves(value), axis=0), preferred_element_type=jnp.float32)
+    return both[: high.shape[0]] + both[high.shape[0] :]
 
 
 def whole_spec():
@@ -105,24 +114,39 @@
 def factor_block(tile):
     lane = lax.broadcasted_iota(jnp.int32, (8, BLK), 1)
     sub = lax.broadcasted_iota(jnp.int32, (8, BLK), 0)
-    groups = [tile[8 * i : 8 * i + 8, :] for i in range(BLK // 8)]
-    for k in range(BLK):
-        here, off = k // 8, k % 8
-        row = jnp.broadcast_to(groups[here][off : off + 1, :], (8, BLK))
-        piv = jnp.broadcast_to(row[:, k : k + 1], (8, BLK))
-        inv = 1.0 / piv
-        unit = jnp.where(lane == k, 1.0, row)
-        scaled = unit * inv
-        for i in range(here, BLK // 8):
-            g = groups[i]
-            col = jnp.broadcast_to(g[:, k : k + 1], (8, BLK))
-            if i == here:
-                col = jnp.where(sub > off, col, 0.0)
-                base = jnp.where((lane == k) & (sub > off), 0.0, g)
-            else:
-                base = jnp.where(lane == k, 0.0, g)
-            groups[i] = base - col * scaled
-    return jnp.concatenate(groups, axis=0)
+    cur = tile
+    done, invs = [], []
+    for p in range(BLK // PANEL):
+        lo = PANEL * p
+        inside = (lane >= lo) & (lane < lo + PANEL)
+        E = {}
+        for i0 in range(0, PANEL, 8):
+            R = cur[i0:i0 + 8, :]
+            for j in range(min(PANEL, i0 + 8)):
+                cj = jnp.broadcast_to(R[:, lo + j : lo + j + 1], (8, BLK))
+                for i in range(max(j, i0), i0 + 8):
+                    E[i, j] = jnp.broadcast_to(cj[i - i0 : i - i0 + 1, :], (8, BLK))
+        rows = [jnp.where(inside, jnp.where(lane == lo + k, 1.0, 0.0), jnp.broadcast_to(cur[k : k + 1, :], (8, BLK))) for k in range(PANEL)]
+        U = [jnp.zeros((8, BLK), jnp.float32)] * (PANEL // 8); I = list(U)
+        for k in range(PANEL):
+            inv = 1.0 / E[k, k]
+            g = k // 8
+            U[g] = jnp.where(sub == k - 8 * g, rows[k], U[g])
+            I[g] = jnp.where(sub == k - 8 * g, inv, I[g])
+            ls = {i: E[i, k] * inv for i in range(k + 1, PANEL)}
+            for i in range(k + 1, PANEL):
+                for j in range(k + 1, i + 1):
+                    E[i, j] = E[i, j] - ls[i] * E[j, k]
+                rows[i] = rows[i] - ls[i] * rows[k]
+        Uc = jnp.concatenate(U, axis=0); Ic = jnp.concatenate(I, axis=0)
+        done.append(Uc); invs.append(Ic)
+        if p < BLK // PANEL - 1:
+            upd = lax.dot_general(Uc, Uc * Ic, (((0,), (0,)), ((), ())), precision=HI, preferred_element_type=jnp.float32)
+            rest = cur[PANEL:, :]
+            lanes = lax.broadcasted_iota(jnp.int32, rest.shape, 1)
+            cur = jnp.where((lanes >= lo) & (lanes < lo + PANEL), 0.0, rest) - upd[lo + PANEL :, :]
+    return jnp.concatenate(done, axis=0), jnp.concatenate(invs, axis=0)
+
 
 def coeff_kernel(s_ref, ch_ref, cl_ref, sh_ref, sl_ref, out_ref, g_ref, p_ref, l_ref):
     n = s_ref.shape[0]
@@ -140,9 +164,8 @@
 
     def step(t, carry):
         start = pl.multiple_of((nb - 1 - t) * BLK, BLK)
-        tile = factor_block(g_ref[pl.ds(start, BLK), pl.ds(start, BLK)])
-        diag = jnp.sum(jnp.where(rr == cc, tile, 0.0), axis=1, keepdims=True)
-        low = jnp.where(cc < rr, tile, jnp.where(rr == cc, 1.0, 0.0)) * lax.rsqrt(diag)
+        tile, invs = factor_block(g_ref[pl.ds(start, BLK), pl.ds(start, BLK)])
+        low = jnp.where(cc <= rr, tile, 0.0) * jnp.sqrt(invs)
         l_ref[pl.ds(start, BLK), :] = low
         panel = jnp.dot(low, g_ref[pl.ds(start, BLK), :], precision=HI, preferred_element_type=jnp.float32)
         p_ref[pl.ds(start, BLK), :] = panel
@@ -279,7 +302,7 @@
     xsq = square(lax.broadcasted_iota(jnp.int32, (BLK, BLK), 1))
     flat = zsq + xsq
     tile = jnp.concatenate([jnp.transpose(ref[...], (1, 0, 2)) for ref in ins], axis=1)
-    spec = mul3((zh[0], zl[0]), halves(jnp.concatenate([tile[j] for j in range(lines)], axis=1)))
+    spec = left3(zh[0], zl[0], jnp.concatenate([tile[j] for j in range(lines)], axis=1))
     scale = 4.0 * math.pi / float(length**3)
     weights = []
     for j in range(lines):
@@ -287,7 +310,7 @@
         safe = jnp.where(total > 0, total, 1.0)
         weights.append(jnp.where(total > 0, scale / safe, 0.0))
     spec = spec * jnp.concatenate(weights, axis=1)
-    back = mul3((zh[1], zl[1]), halves(spec))
+    back = left3(zh[1], zl[1], spec)
     back = jnp.stack([back[:, j * BLK : (j + 1) * BLK] for j in range(lines)], axis=0)
     start = 0
     for ref in outs:
@@ -296,7 +319,7 @@
         start += part
 
 
-def columns(ztab, values, lines=8):
+def columns(ztab, values, lines=16):
     count = len(values)
     specs = [pl.BlockSpec((v.shape[0], lines, BLK), lambda i: (0, i, 0)) for v in values]
     table = pl.BlockSpec((2, BLK, BLK), lambda i: (0, 0, 0))

time: 440 us -> 373 us (0.85)
  Pallas kernels: 190 us -> 128 us
  waiting for transfers between devices: 136 us -> 173 us
  blocking collectives: 73.8 us -> 37.5 us
    pallas_call x1, Pallas kernels: 77.8 us -> 33 us  [coefficients(): pl.pallas_call(coeff_kernel, out_shape=[coeff, coeff, sample, sample], sc...]
    all_to_all x5 -> x4, waiting for transfers between devices: 136 us -> 173 us  [exchange(): return lax.all_to_all(blocks, AXES, split_axis=0, concat_axis=0, tiled=True)]
    all_to_all x3 -> x2, blocking collectives: 73.8 us -> 37.5 us  [exchange(): return lax.all_to_all(blocks, AXES, split_axis=0, concat_axis=0, tiled=True)]
    pallas_call x6 -> x4, Pallas kernels: 38.8 us -> 30.6 us  [planes(): pl.pallas_call(kernel, out_shape=jax.ShapeDtypeStruct(out_shape, jnp.floa...]
    pallas_call x1, Pallas kernels: 17.8 us -> 12.5 us  [columns(): pl.pallas_call(functools.partial(columns_kernel, count), out_shape=[jax.S...]
    all_to_all x5 -> x4, starting transfers between devices: 25.8 us -> 23.5 us  [exchange(): return lax.all_to_all(blocks, AXES, split_axis=0, concat_axis=0, tiled=True)]
    pallas_call x3 -> x2, Pallas kernels: 33.7 us -> 31.4 us  [fit(): pl.pallas_call(fit_kernel, out_shape=jax.ShapeDtypeStruct((vectors, count...]
    pallas_call x3 -> x2, Pallas kernels: 10.1 us -> 8.45 us  [join(): pl.pallas_call(functools.partial(join_kernel, first), out_shape=jax.Shape...]
  transfers between devices with their start and end apart: 5 -> 4, of which waited for: 5 -> 4; matrix products, arithmetic and copies ran while one was open for 1% -> 1% of each run, Pallas kernels for 13% -> 9%
where the time goes in v4:
time: 373 us; the launch traced here: 371 us
  waiting for transfers between devices  173 us (46%)
  Pallas kernels  128 us (34%)
  blocking collectives  37.5 us (10%)
  starting transfers between devices  23.5 us (6%)
  other arithmetic  5.63 us (2%)
  local copies, waits for them, and re-layouts  3.85 us (1%)
    all_to_all x4, waiting for transfers between devices, exchange(): return lax.all_to_all(blocks, AXES, split_axis=0, concat_axis=0, tiled=True)  173 us
    all_to_all x2, blocking collectives, exchange(): return lax.all_to_all(blocks, AXES, split_axis=0, concat_axis=0, tiled=True)  37.5 us
    pallas_call x1, Pallas kernels, coefficients(): pl.pallas_call(coeff_kernel, out_shape=[coeff, coeff, sample, sample], sc...  33 us
    pallas_call x2, Pallas kernels, fit(): pl.pallas_call(fit_kernel, out_shape=jax.ShapeDtypeStruct((vectors, count...  31.4 us
    pallas_call x4, Pallas kernels, planes(): pl.pallas_call(kernel, out_shape=jax.ShapeDtypeStruct(out_shape, jnp.floa...  30.6 us
    all_to_all x4, starting transfers between devices, exchange(): return lax.all_to_all(blocks, AXES, split_axis=0, concat_axis=0, tiled=True)  23.5 us
    pallas_call x1, Pallas kernels, columns(): pl.pallas_call(functools.partial(columns_kernel, count), out_shape=[jax.S...  12.5 us
    pallas_call x1, Pallas kernels, pick(): pl.pallas_call(pick_kernel, out_shape=jax.ShapeDtypeStruct((npoint, norbi...  12 us
  transfers between devices with their start and end apart: 4, of which 4 were waited for; matrix products, arithmetic and copies ran while one was open for 1% of the time, Pallas kernels for 9%

profile of v4, /device:TPU:0, one launch (start us, length us, event | category | flops | bytes accessed | tf_op | source)
XLA Modules:
  0.0 371.4 jit_solution(12444067851479304624)
XLA Ops:
  0.0 0.7 add_select_fusion.5
  0.7 0.7 and_convert_fusion
  1.4 0.6 pad_add_fusion.info
  2.0 12.0 %pick.1 = f32[512,256]{1,0:T(8,128)} custom-call(s32[4,512]{1,0:T(4,128)} %pad_add_fusion.info, f32[256,32,4,128]{3,2,1,0:T(4,128)} %orb.1), custom_call_target="tpu_custom_call" | custom-call | tf_op jit(solution)/shard_map/pick/pallas_call | solution.py:99
  14.0 1.2 reshape.107
  15.2 19.4 %all_to_all.30 = f32[128,4,256]{2,1,0:T(4,128)S(1)} all-to-all(f32[128,4,256]{2,1,0:T(4,128)S(1)} %reshape.107), channel_id=1, replica_groups=mesh['slab'=4,'wide'=32] {'slab','wide'}, dimensions={0} | all-to-all | bytes 1048576 | tf_op jit(solution)/shard_map/all_to_all | solution.py:27
  34.9 18.1 %all_to_all.31 = f32[128,4,256]{2,1,0:T(4,128)S(1)} all-to-all(f32[128,4,256]{2,1,0:T(4,128)S(1)} %broadcast_in_dim.2), channel_id=1, replica_groups=mesh['slab'=4,'wide'=32] {'slab','wide'}, dimensions={0} | all-to-all | bytes 1048576 | tf_op jit(solution)/shard_map/all_to_all | solution.py:27
  52.9 1.0 reshape.108.s_ref
  53.9 33.0 %coefficients.1 = (bf16[128,512]{1,0:T(8,128)(2,1)}, bf16[128,512]{1,0:T(8,128)(2,1)}, bf16[512,256]{1,0:T(8,128)(2,1)}, bf16[512,256]{1,0:T(8,128)(2,1)}) custom-call(f32[512,256]{1,0:T(8,128)} %reshape.108.s_ref), custom_call_target="tpu_custom_call" | custom-call | tf_op jit(solution)/shard_map/coefficients/pallas_call | solution.py:192
  86.9 15.6 %fit.2 = f32[128,64,128]{2,1,0:T(8,128)} custom-call(bf16[512,256]{1,0:T(8,128)(2,1)} %get-tuple-element.14.sh, bf16[512,256]{1,0:T(8,128)(2,1)} %get-tuple-element.15.sl, bf16[128,512]{1,0:T(8,128)(2,1)} %get-tuple-element.16.ch, bf16[128,512]{1,0:T(8,128)(2,1)} %get-tuple-element.17.cl, f32[256,128,128]{2,1,0:T(8,128)} %bitcast.41), custom_call_target="tpu_custom_call" | custom-call | flops 9663676416 | bytes 12582912 | tf_op jit(solution)/shard_map/fit/pallas_call | solution.py:223
  102.5 6.0 %all-to-all-start.2 = ((f32[128,64,128]{2,1,0:T(8,128)}), f32[128,64,128]{2,1,0:T(8,128)}, u32[]{:S(2)}, u32[]{:S(2)}) async-start(f32[128,64,128]{2,1,0:T(8,128)} %fit.2), calls=%async_computation.2 | async-start | bytes 8388608 | tf_op jit(solution)/shard_map/all_to_all | solution.py:27
  108.5 15.8 %fit.3 = f32[128,64,128]{2,1,0:T(8,128)} custom-call(bf16[512,256]{1,0:T(8,128)(2,1)} %get-tuple-element.14.sh, bf16[512,256]{1,0:T(8,128)(2,1)} %get-tuple-element.15.sl, bf16[128,512]{1,0:T(8,128)(2,1)} %get-tuple-element.16.ch, bf16[128,512]{1,0:T(8,128)(2,1)} %get-tuple-element.17.cl, f32[256,128,128]{2,1,0:T(8,128)} %bitcast.42), custom_call_target="tpu_custom_call" | custom-call | flops 9663676416 | bytes 12582912 | tf_op jit(solution)/shard_map/fit/pallas_call | solution.py:223
  124.3 37.4 %all-to-all-done.2 = f32[128,64,128]{2,1,0:T(8,128)} async-done(((f32[128,64,128]{2,1,0:T(8,128)}), f32[128,64,128]{2,1,0:T(8,128)}, u32[]{:S(2)}, u32[]{:S(2)}) %all-to-all-start.2) | async-done | bytes 4194336 | tf_op jit(solution)/shard_map/all_to_all | solution.py:27
  161.7 5.8 %all-to-all-start.3 = ((f32[128,64,128]{2,1,0:T(8,128)}), f32[128,64,128]{2,1,0:T(8,128)}, u32[]{:S(2)}, u32[]{:S(2)}) async-start(f32[128,64,128]{2,1,0:T(8,128)} %fit.3), calls=%async_computation.3 | async-start | bytes 8388608 | tf_op jit(solution)/shard_map/all_to_all | solution.py:27
  168.0 0.6 sine_add_fusion.1
  168.8 0.8 copy.6.yl
  169.6 0.8 copy.5.yh
  170.3 0.9 reduce-precision_convert_fusion.3
  171.3 0.7 fusion.2
  171.9 0.7 fusion
  172.7 8.2 %planes_in.2 = f32[4,16,128,128]{3,2,1,0:T(8,128)} custom-call(bf16[128,128]{1,0:T(8,128)(2,1)} %get-tuple-element.37.xh, bf16[128,128]{1,0:T(8,128)(2,1)} %get-tuple-element.38.xl, bf16[256,256]{1,0:T(8,128)(2,1)} %copy.5.yh, bf16[256,256]{1,0:T(8,128)(2,1)} %copy.6.yl, f32[4,32,64,128]{3,2,1,0:T(8,128)} %bitcast.11.in_ref), custom_call_target="tpu_custom_call" | custom-call | flops 2415919104 | bytes 8388608 | tf_op jit(solution)/shard_map/planes_in/pallas_call | solution.py:277
  180.8 40.0 %all-to-all-done.3 = f32[128,64,128]{2,1,0:T(8,128)} async-done(((f32[128,64,128]{2,1,0:T(8,128)}), f32[128,64,128]{2,1,0:T(8,128)}, u32[]{:S(2)}, u32[]{:S(2)}) %all-to-all-start.3) | async-done | bytes 4194336 | tf_op jit(solution)/shard_map/all_to_all | solution.py:27
  220.9 8.2 %planes_in.3 = f32[4,16,128,128]{3,2,1,0:T(8,128)} custom-call(bf16[128,128]{1,0:T(8,128)(2,1)} %get-tuple-element.37.xh, bf16[128,128]{1,0:T(8,128)(2,1)} %get-tuple-element.38.xl, bf16[256,256]{1,0:T(8,128)(2,1)} %copy.5.yh, bf16[256,256]{1,0:T(8,128)(2,1)} %copy.6.yl, f32[4,32,64,128]{3,2,1,0:T(8,128)} %bitcast.13.in_ref), custom_call_target="tpu_custom_call" | custom-call | flops 2415919104 | bytes 8388608 | tf_op jit(solution)/shard_map/planes_in/pallas_call | solution.py:277
  229.1 12.5 %columns.1 = (f32[64,128,128]{2,1,0:T(8,128)}, f32[64,128,128]{2,1,0:T(8,128)}) custom-call(bf16[2,128,128]{2,1,0:T(8,128)(2,1)} %get-tuple-element.30.zh, bf16[2,128,128]{2,1,0:T(8,128)(2,1)} %get-tuple-element.29.zl, f32[64,128,128]{2,1,0:T(8,128)} %bitcast.54, f32[64,128,128]{2,1,0:T(8,128)} %bitcast.55), custom_call_target="tpu_custom_call" | custom-call | flops 3221225472 | bytes 16777216 | tf_op jit(solution)/shard_map/columns/pallas_call | solution.py:327
  241.5 7.1 %planes_out.3 = f32[4,32,64,128]{3,2,1,0:T(8,128)} custom-call(bf16[128,128]{1,0:T(8,128)(2,1)} %get-tuple-element.37.xh, bf16[128,128]{1,0:T(8,128)(2,1)} %get-tuple-element.38.xl, bf16[256,256]{1,0:T(8,128)(2,1)} %get-tuple-element.28.yh, bf16[256,256]{1,0:T(8,128)(2,1)} %get-tuple-element.27.yl, f32[4,16,128,128]{3,2,1,0:T(8,128)} %bitcast.56), custom_call_target="tpu_custom_call" | custom-call | flops 2415919104 | bytes 8388608 | tf_op jit(solution)/shard_map/planes_out/pallas_call | solution.py:277
  248.6 5.8 %all-to-all-start.5 = ((f32[128,64,128]{2,1,0:T(8,128)}), f32[128,64,128]{2,1,0:T(8,128)}, u32[]{:S(2)}, u32[]{:S(2)}) async-start(f32[128,64,128]{2,1,0:T(8,128)} %bitcast.44), calls=%async_computation.5 | async-start | bytes 8388608 | tf_op jit(solution)/shard_map/all_to_all | solution.py:27
  254.5 7.1 %planes_out.2 = f32[4,32,64,128]{3,2,1,0:T(8,128)} custom-call(bf16[128,128]{1,0:T(8,128)(2,1)} %get-tuple-element.37.xh, bf16[128,128]{1,0:T(8,128)(2,1)} %get-tuple-element.38.xl, bf16[256,256]{1,0:T(8,128)(2,1)} %get-tuple-element.28.yh, bf16[256,256]{1,0:T(8,128)(2,1)} %get-tuple-element.27.yl, f32[4,16,128,128]{3,2,1,0:T(8,128)} %bitcast.53), custom_call_target="tpu_custom_call" | custom-call | flops 2415919104 | bytes 8388608 | tf_op jit(solution)/shard_map/planes_out/pallas_call | solution.py:277
  261.6 46.2 %all-to-all-done.5 = f32[128,64,128]{2,1,0:T(8,128)} async-done(((f32[128,64,128]{2,1,0:T(8,128)}), f32[128,64,128]{2,1,0:T(8,128)}, u32[]{:S(2)}, u32[]{:S(2)}) %all-to-all-start.5) | async-done | bytes 4194336 | tf_op jit(solution)/shard_map/all_to_all | solution.py:27
  307.8 5.8 %all-to-all-start.4 = ((f32[128,64,128]{2,1,0:T(8,128)}), f32[128,64,128]{2,1,0:T(8,128)}, u32[]{:S(2)}, u32[]{:S(2)}) async-start(f32[128,64,128]{2,1,0:T(8,128)} %bitcast.43), calls=%async_computation.4 | async-start | bytes 8388608 | tf_op jit(solution)/shard_map/all_to_all | solution.py:27
  313.6 4.2 %join.2.refs_0_ = f32[128,32,4,128]{3,2,1,0:T(4,128)} custom-call(f32[128,16,4,128]{3,2,1,0:T(4,128)} %bitcast.20.src), custom_call_target="tpu_custom_call" | custom-call | bytes 8388608 | tf_op jit(solution)/shard_map/join/pallas_call | solution.py:360
  317.9 49.1 %all-to-all-done.4 = f32[128,64,128]{2,1,0:T(8,128)} async-done(((f32[128,64,128]{2,1,0:T(8,128)}), f32[128,64,128]{2,1,0:T(8,128)}, u32[]{:S(2)}, u32[]{:S(2)}) %all-to-all-start.4) | async-done | bytes 4194336 | tf_op jit(solution)/shard_map/all_to_all | solution.py:27
  367.0 4.2 %join.3 = f32[128,32,4,128]{3,2,1,0:T(4,128)} custom-call(f32[128,16,4,128]{3,2,1,0:T(4,128)} %bitcast.17.src, f32[128,32,4,128]{3,2,1,0:T(4,128)} %join.2.refs_0_), custom_call_target="tpu_custom_call", output_to_operand_aliasing={{}: (1, {})} | custom-call | bytes 8388608 | tf_op jit(solution)/shard_map/join/pallas_call | solution.py:360
  (12 shorter events, 0.9 us)
Async XLA Ops:
  102.5 59.2 %all-to-all-start.2 = ((f32[128,64,128]{2,1,0:T(8,128)}), f32[128,64,128]{2,1,0:T(8,128)}, u32[]{:S(2)}, u32[]{:S(2)}) async-start(f32[128,64,128]{2,1,0:T(8,128)} %fit.2), calls=%async_computation.2 | async-start | bytes 8388608 | tf_op jit(solution)/shard_map/all_to_all | solution.py:27
  161.7 59.2 %all-to-all-start.3 = ((f32[128,64,128]{2,1,0:T(8,128)}), f32[128,64,128]{2,1,0:T(8,128)}, u32[]{:S(2)}, u32[]{:S(2)}) async-start(f32[128,64,128]{2,1,0:T(8,128)} %fit.3), calls=%async_computation.3 | async-start | bytes 8388608 | tf_op jit(solution)/shard_map/all_to_all | solution.py:27
  248.6 59.2 %all-to-all-start.5 = ((f32[128,64,128]{2,1,0:T(8,128)}), f32[128,64,128]{2,1,0:T(8,128)}, u32[]{:S(2)}, u32[]{:S(2)}) async-start(f32[128,64,128]{2,1,0:T(8,128)} %bitcast.44), calls=%async_computation.5 | async-start | bytes 8388608 | tf_op jit(solution)/shard_map/all_to_all | solution.py:27
  307.8 59.2 %all-to-all-start.4 = ((f32[128,64,128]{2,1,0:T(8,128)}), f32[128,64,128]{2,1,0:T(8,128)}, u32[]{:S(2)}, u32[]{:S(2)}) async-start(f32[128,64,128]{2,1,0:T(8,128)} %bitcast.43), calls=%async_computation.4 | async-start | bytes 8388608 | tf_op jit(solution)/shard_map/all_to_all | solution.py:27

commit v5 on v4

--- a/solution.py
+++ b/solution.py
@@ -11,7 +11,7 @@
 AXES = ("slab", "wide")
 HI = lax.Precision.HIGHEST
 BLK = 128
-PARTS = (16, 16)
+PARTS = (12, 20)
 SLOTS = 8
 PANEL = 16
 
@@ -42,6 +42,12 @@
         return jnp.dot(a, b, preferred_element_type=jnp.float32)
 
     return one(left[0], right[0]) + (one(left[1], right[0]) + one(left[0], right[1]))
+
+
+def stacked3(left, right):
+    size = left[0].shape[0]
+    both = jnp.dot(jnp.concatenate(left, axis=0), right[0], preferred_element_type=jnp.float32)
+    return both[:size] + (both[size:] + jnp.dot(left[0], right[1], preferred_element_type=jnp.float32))
 
 
 def left3(high, low, value):
@@ -59,13 +65,12 @@
 def pick_kernel(info, orb, out_ref, buf, acc, order, sems):
     npoint = info.shape[1]
     lane = lax.broadcasted_iota(jnp.int32, (acc.shape[0], BLK), 1)
-    acc[...] = jnp.zeros_like(acc)
 
     def collect(m, count):
         order[count] = m
         return count + info[0, m]
 
-    total = lax.fori_loop(0, npoint, collect, 0)
+    total = lax.fori_loop(0, npoint, collect, 0, unroll=16)
 
     def copy(i):
         m = order[i]
@@ -75,6 +80,8 @@
     @pl.loop(0, jnp.minimum(total, SLOTS - 1))
     def _(i):
         copy(i).start()
+
+    acc[...] = jnp.zeros_like(acc)
 
     @pl.loop(0, total)
     def _(i):
@@ -210,8 +217,8 @@
         top, low = halves(turned[r])
         bh[:, r * BLK : (r + 1) * BLK] = top
         bl[:, r * BLK : (r + 1) * BLK] = low
-    pairs = mul3((sh[...], sl[...]), (bh[...], bl[...]))
-    piece = mul3((ch[...], cl[...]), halves(pairs * pairs))
+    pairs = stacked3((sh[...], sl[...]), (bh[...], bl[...]))
+    piece = stacked3((ch[...], cl[...]), halves(pairs * pairs))
     piece = jnp.stack([piece[:, r * BLK : (r + 1) * BLK] for r in range(lines)], axis=0)
     out_ref[...] = jnp.transpose(piece, (1, 0, 2))
 
@@ -247,12 +254,13 @@
 
 def planes_in_kernel(xh, xl, yh, yl, in_ref, out_ref):
     pairs = in_ref.shape[2] // 8
-    for p in range(0, pairs, 4):
-        tall = [in_ref[0, :, 8 * (p + g) : 8 * (p + g) + 8, :].reshape(2 * BLK, BLK) for g in range(4)]
+    group = pairs // 2
+    for p in range(0, pairs, group):
+        tall = [in_ref[0, :, 8 * (p + g) : 8 * (p + g) + 8, :].reshape(2 * BLK, BLK) for g in range(group)]
         along = mul3(halves(jnp.concatenate(tall, axis=0)), (xh[...], xl[...]))
-        wide = [along[2 * BLK * g : 2 * BLK * (g + 1)] for g in range(4)]
+        wide = [along[2 * BLK * g : 2 * BLK * (g + 1)] for g in range(group)]
         both = mul3((yh[...], yl[...]), halves(jnp.concatenate(wide, axis=1)))
-        for g in range(4):
+        for g in range(group):
             out_ref[0, 2 * (p + g)] = both[:BLK, BLK * g : BLK * (g + 1)]
             out_ref[0, 2 * (p + g) + 1] = both[BLK:, BLK * g : BLK * (g + 1)]
 
@@ -287,8 +295,8 @@
     )(*xtab, *ytab, values)
 
 
-def columns_kernel(count, zh, zl, *refs):
-    ins, outs = refs[:count], refs[count:]
+def columns_kernel(start, zh, zl, *refs):
+    ins, out = refs[:-1], refs[-1]
     lines = ins[0].shape[1]
     base = pl.program_id(0) * lines
     length = BLK
@@ -310,29 +318,24 @@
         safe = jnp.where(total > 0, total, 1.0)
         weights.append(jnp.where(total > 0, scale / safe, 0.0))
     spec = spec * jnp.concatenate(weights, axis=1)
-    back = left3(zh[1], zl[1], spec)
+    part = out.shape[0]
+    back = left3(zh[1, start : start + part], zl[1, start : start + part], spec)
     back = jnp.stack([back[:, j * BLK : (j + 1) * BLK] for j in range(lines)], axis=0)
-    start = 0
-    for ref in outs:
-        part = ref.shape[0]
-        ref[...] = jnp.transpose(back[:, start : start + part], (1, 0, 2))
-        start += part
-
-
-def columns(ztab, values, lines=16):
-    count = len(values)
+    out[...] = jnp.transpose(back, (1, 0, 2))
+
+
+def columns(ztab, values, which, lines=16):
+    start = sum(v.shape[0] for v in values[:which])
     specs = [pl.BlockSpec((v.shape[0], lines, BLK), lambda i: (0, i, 0)) for v in values]
     table = pl.BlockSpec((2, BLK, BLK), lambda i: (0, 0, 0))
     size = BLK**3
     return pl.pallas_call(
-        functools.partial(columns_kernel, count),
-        out_shape=[jax.ShapeDtypeStruct(v.shape, jnp.float32) for v in values],
+        functools.partial(columns_kernel, start),
+        out_shape=jax.ShapeDtypeStruct(values[which].shape, jnp.float32),
         grid=(BLK // lines,),
         in_specs=[table, table] + specs,
-        out_specs=specs,
-        cost_estimate=pl.CostEstimate(
-            flops=12 * size * BLK, transcendentals=size, bytes_accessed=8 * size
-        ),
+        out_specs=specs[which],
+        cost_estimate=pl.CostEstimate(flops=9 * size * BLK, transcendentals=size, bytes_accessed=6 * size),
         name="columns",
     )(*ztab, *values)
 
@@ -408,10 +411,9 @@
         whole = exchange(piece).reshape(slabs, wides, part * rows, grid)
         spec = planes(planes_in_kernel, xtab, yin, whole, (slabs, part, grid, grid), "planes_in")
         spectra.append(spec.reshape(slabs * part, grid, grid))
-    spectra = columns(ztab, spectra)
     out = None
-    for spec, lo, part in zip(spectra, starts, PARTS):
-        spec = spec.reshape(slabs, part, grid, grid)
+    for c, (lo, part) in enumerate(zip(starts, PARTS)):
+        spec = columns(ztab, spectra, c).reshape(slabs, part, grid, grid)
         back = planes(planes_out_kernel, xtab, yout, spec, (slabs, wides, part * rows, grid), "planes_out")
         piece = exchange(back.reshape(devices, part * rows, grid)).reshape(devices, part, rows, grid)
         out = join(piece, out, lo, (devices, depth, rows, grid))

time: 373 us -> 371 us (level)
  waiting for transfers between devices: 173 us -> 157 us
  Pallas kernels: 128 us -> 139 us
    all_to_all x4, waiting for transfers between devices: 173 us -> 157 us  [exchange(): return lax.all_to_all(blocks, AXES, split_axis=0, concat_axis=0, tiled=True)]
    pallas_call x1 -> x2, Pallas kernels: 12.5 us -> 22.7 us  [columns(): pl.pallas_call(functools.partial(columns_kernel, start), out_shape=jax.Sh...]
    pallas_call x4, Pallas kernels: 30.6 us -> 35.8 us  [planes(): pl.pallas_call(kernel, out_shape=jax.ShapeDtypeStruct(out_shape, jnp.floa...]
  transfers between devices with their start and end apart: 4 -> 4, of which waited for: 4 -> 4; matrix products, arithmetic and copies ran while one was open for 1% -> 1% of each run, Pallas kernels for 9% -> 14%
where the time goes in v5:
time: 371 us; the launch traced here: 370 us
  waiting for transfers between devices  157 us (42%)
  Pallas kernels  139 us (37%)
  blocking collectives  38.5 us (10%)
  starting transfers between devices  21.5 us (6%)
  local copies, waits for them, and re-layouts  7.3 us (2%)
  other arithmetic  5.62 us (2%)
    all_to_all x4, waiting for transfers between devices, exchange(): return lax.all_to_all(blocks, AXES, split_axis=0, concat_axis=0, tiled=True)  157 us
    all_to_all x2, blocking collectives, exchange(): return lax.all_to_all(blocks, AXES, split_axis=0, concat_axis=0, tiled=True)  38.5 us
    pallas_call x4, Pallas kernels, planes(): pl.pallas_call(kernel, out_shape=jax.ShapeDtypeStruct(out_shape, jnp.floa...  35.8 us
    pallas_call x1, Pallas kernels, coefficients(): pl.pallas_call(coeff_kernel, out_shape=[coeff, coeff, sample, sample], sc...  33 us
    pallas_call x2, Pallas kernels, fit(): pl.pallas_call(fit_kernel, out_shape=jax.ShapeDtypeStruct((vectors, count...  30 us
    pallas_call x2, Pallas kernels, columns(): pl.pallas_call(functools.partial(columns_kernel, start), out_shape=jax.Sh...  22.7 us
    all_to_all x4, starting transfers between devices, exchange(): return lax.all_to_all(blocks, AXES, split_axis=0, concat_axis=0, tiled=True)  21.5 us
    pallas_call x1, Pallas kernels, pick(): pl.pallas_call(pick_kernel, out_shape=jax.ShapeDtypeStruct((npoint, norbi...  9.27 us
  transfers between devices with their start and end apart: 4, of which 4 were waited for; matrix products, arithmetic and copies ran while one was open for 1% of the time, Pallas kernels for 14%

profile of v5, /device:TPU:0, one launch (start us, length us, event | category | flops | bytes accessed | tf_op | source)
XLA Modules:
  0.0 369.5 jit_solution(4096557853835523151)
XLA Ops:
  0.0 0.7 add_select_fusion.5
  0.7 0.7 and_convert_fusion
  2.0 9.3 %pick.1 = f32[512,256]{1,0:T(8,128)} custom-call(s32[4,512]{1,0:T(4,128)} %pad_add_fusion.info, f32[256,32,4,128]{3,2,1,0:T(4,128)} %orb.1), custom_call_target="tpu_custom_call" | custom-call | tf_op jit(solution)/shard_map/pick/pallas_call | solution.py:106
  11.3 1.2 reshape.107
  12.5 20.5 %all_to_all.30 = f32[128,4,256]{2,1,0:T(4,128)S(1)} all-to-all(f32[128,4,256]{2,1,0:T(4,128)S(1)} %reshape.107), channel_id=1, replica_groups=mesh['slab'=4,'wide'=32] {'slab','wide'}, dimensions={0} | all-to-all | bytes 1048576 | tf_op jit(solution)/shard_map/all_to_all | solution.py:27
  33.2 18.1 %all_to_all.31 = f32[128,4,256]{2,1,0:T(4,128)S(1)} all-to-all(f32[128,4,256]{2,1,0:T(4,128)S(1)} %broadcast_in_dim.2), channel_id=1, replica_groups=mesh['slab'=4,'wide'=32] {'slab','wide'}, dimensions={0} | all-to-all | bytes 1048576 | tf_op jit(solution)/shard_map/all_to_all | solution.py:27
  51.3 1.0 reshape.108.s_ref
  52.2 33.0 %coefficients.1 = (bf16[128,512]{1,0:T(8,128)(2,1)}, bf16[128,512]{1,0:T(8,128)(2,1)}, bf16[512,256]{1,0:T(8,128)(2,1)}, bf16[512,256]{1,0:T(8,128)(2,1)}) custom-call(f32[512,256]{1,0:T(8,128)} %reshape.108.s_ref), custom_call_target="tpu_custom_call" | custom-call | tf_op jit(solution)/shard_map/coefficients/pallas_call | solution.py:199
  85.2 11.8 %fit.2 = f32[128,48,128]{2,1,0:T(8,128)} custom-call(bf16[512,256]{1,0:T(8,128)(2,1)} %get-tuple-element.12.sh, bf16[512,256]{1,0:T(8,128)(2,1)} %get-tuple-element.13.sl, bf16[128,512]{1,0:T(8,128)(2,1)} %get-tuple-element.14.ch, bf16[128,512]{1,0:T(8,128)(2,1)} %get-tuple-element.15.cl, f32[256,128,128]{2,1,0:T(8,128)} %bitcast.43), custom_call_target="tpu_custom_call" | custom-call | flops 7247757312 | bytes 9437184 | tf_op jit(solution)/shard_map/fit/pallas_call | solution.py:230
  97.0 4.8 %all-to-all-start.2 = ((f32[128,48,128]{2,1,0:T(8,128)}), f32[128,48,128]{2,1,0:T(8,128)S(1)}, u32[]{:S(2)}, u32[]{:S(2)}) async-start(f32[128,48,128]{2,1,0:T(8,128)} %fit.2), calls=%async_computation.2 | async-start | bytes 6291456 | tf_op jit(solution)/shard_map/all_to_all | solution.py:27
  101.9 18.2 %fit.3 = f32[128,80,128]{2,1,0:T(8,128)} custom-call(bf16[512,256]{1,0:T(8,128)(2,1)} %get-tuple-element.12.sh, bf16[512,256]{1,0:T(8,128)(2,1)} %get-tuple-element.13.sl, bf16[128,512]{1,0:T(8,128)(2,1)} %get-tuple-element.14.ch, bf16[128,512]{1,0:T(8,128)(2,1)} %get-tuple-element.15.cl, f32[256,128,128]{2,1,0:T(8,128)} %bitcast.44), custom_call_target="tpu_custom_call" | custom-call | flops 12079595520 | bytes 15728640 | tf_op jit(solution)/shard_map/fit/pallas_call | solution.py:230
  120.1 23.2 %all-to-all-done.2 = f32[128,48,128]{2,1,0:T(8,128)S(1)} async-done(((f32[128,48,128]{2,1,0:T(8,128)}), f32[128,48,128]{2,1,0:T(8,128)S(1)}, u32[]{:S(2)}, u32[]{:S(2)}) %all-to-all-start.2) | async-done | bytes 3145760 | tf_op jit(solution)/shard_map/all_to_all | solution.py:27
  143.3 1.7 copy-done.1
  145.0 5.8 %all-to-all-start.3 = ((f32[128,80,128]{2,1,0:T(8,128)}), f32[128,80,128]{2,1,0:T(8,128)}, u32[]{:S(2)}, u32[]{:S(2)}) async-start(f32[128,80,128]{2,1,0:T(8,128)} %fit.3), calls=%async_computation.3 | async-start | bytes 10485760 | tf_op jit(solution)/shard_map/all_to_all | solution.py:27
  152.1 0.8 copy.11.yl
  152.9 0.8 copy.10.yh
  153.6 0.9 reduce-precision_convert_fusion.3
  155.2 0.7 fusion
  156.0 8.7 %planes_in.2 = f32[4,12,128,128]{3,2,1,0:T(8,128)} custom-call(bf16[128,128]{1,0:T(8,128)(2,1)} %get-tuple-element.29.xh, bf16[128,128]{1,0:T(8,128)(2,1)} %get-tuple-element.30.xl, bf16[256,256]{1,0:T(8,128)(2,1)} %copy.10.yh, bf16[256,256]{1,0:T(8,128)(2,1)} %copy.11.yl, f32[4,32,48,128]{3,2,1,0:T(8,128)} %bitcast.50), custom_call_target="tpu_custom_call" | custom-call | flops 1811939328 | bytes 6291456 | tf_op jit(solution)/shard_map/planes_in/pallas_call | solution.py:285
  164.6 51.2 %all-to-all-done.3 = f32[128,80,128]{2,1,0:T(8,128)} async-done(((f32[128,80,128]{2,1,0:T(8,128)}), f32[128,80,128]{2,1,0:T(8,128)}, u32[]{:S(2)}, u32[]{:S(2)}) %all-to-all-start.3) | async-done | bytes 5242912 | tf_op jit(solution)/shard_map/all_to_all | solution.py:27
  215.8 11.6 %planes_in.3 = f32[4,20,128,128]{3,2,1,0:T(8,128)} custom-call(bf16[128,128]{1,0:T(8,128)(2,1)} %get-tuple-element.29.xh, bf16[128,128]{1,0:T(8,128)(2,1)} %get-tuple-element.30.xl, bf16[256,256]{1,0:T(8,128)(2,1)} %copy.10.yh, bf16[256,256]{1,0:T(8,128)(2,1)} %copy.11.yl, f32[4,32,80,128]{3,2,1,0:T(8,128)} %bitcast.11.in_ref), custom_call_target="tpu_custom_call" | custom-call | flops 3019898880 | bytes 10485760 | tf_op jit(solution)/shard_map/planes_in/pallas_call | solution.py:285
  227.5 11.0 %columns.3 = f32[48,128,128]{2,1,0:T(8,128)} custom-call(bf16[2,128,128]{2,1,0:T(8,128)(2,1)} %get-tuple-element.26.zh, bf16[2,128,128]{2,1,0:T(8,128)(2,1)} %get-tuple-element.25.zl, f32[48,128,128]{2,1,0:T(8,128)} %bitcast.46, f32[80,128,128]{2,1,0:T(8,128)} %bitcast.41), custom_call_target="tpu_custom_call" | custom-call | flops 2415919104 | bytes 12582912 | tf_op jit(solution)/shard_map/columns/pallas_call | solution.py:332
  238.5 6.7 %planes_out.3 = f32[4,32,48,128]{3,2,1,0:T(8,128)} custom-call(bf16[128,128]{1,0:T(8,128)(2,1)} %get-tuple-element.29.xh, bf16[128,128]{1,0:T(8,128)(2,1)} %get-tuple-element.30.xl, bf16[256,256]{1,0:T(8,128)(2,1)} %get-tuple-element.24.yh, bf16[256,256]{1,0:T(8,128)(2,1)} %get-tuple-element.23.yl, f32[4,12,128,128]{3,2,1,0:T(8,128)} %bitcast.52), custom_call_target="tpu_custom_call" | custom-call | flops 1811939328 | bytes 6291456 | tf_op jit(solution)/shard_map/planes_out/pallas_call | solution.py:285
  245.2 5.0 %all-to-all-start.5 = ((f32[128,48,128]{2,1,0:T(8,128)}), f32[128,48,128]{2,1,0:T(8,128)S(1)}, u32[]{:S(2)}, u32[]{:S(2)}) async-start(f32[128,48,128]{2,1,0:T(8,128)} %bitcast.51), calls=%async_computation.5 | async-start | bytes 6291456 | tf_op jit(solution)/shard_map/all_to_all | solution.py:27
  250.2 11.7 %columns.2 = f32[80,128,128]{2,1,0:T(8,128)} custom-call(bf16[2,128,128]{2,1,0:T(8,128)(2,1)} %get-tuple-element.26.zh, bf16[2,128,128]{2,1,0:T(8,128)(2,1)} %get-tuple-element.25.zl, f32[48,128,128]{2,1,0:T(8,128)} %bitcast.47, f32[80,128,128]{2,1,0:T(8,128)} %bitcast.42), custom_call_target="tpu_custom_call" | custom-call | flops 2415919104 | bytes 12582912 | tf_op jit(solution)/shard_map/columns/pallas_call | solution.py:332
  261.9 8.8 %planes_out.2 = f32[4,32,80,128]{3,2,1,0:T(8,128)} custom-call(bf16[128,128]{1,0:T(8,128)(2,1)} %get-tuple-element.29.xh, bf16[128,128]{1,0:T(8,128)(2,1)} %get-tuple-element.30.xl, bf16[256,256]{1,0:T(8,128)(2,1)} %get-tuple-element.24.yh, bf16[256,256]{1,0:T(8,128)(2,1)} %get-tuple-element.23.yl, f32[4,20,128,128]{3,2,1,0:T(8,128)} %bitcast.49), custom_call_target="tpu_custom_call" | custom-call | flops 3019898880 | bytes 10485760 | tf_op jit(solution)/shard_map/planes_out/pallas_call | solution.py:285
  270.8 21.1 %all-to-all-done.5 = f32[128,48,128]{2,1,0:T(8,128)S(1)} async-done(((f32[128,48,128]{2,1,0:T(8,128)}), f32[128,48,128]{2,1,0:T(8,128)S(1)}, u32[]{:S(2)}, u32[]{:S(2)}) %all-to-all-start.5) | async-done | bytes 3145760 | tf_op jit(solution)/shard_map/all_to_all | solution.py:27
  291.8 1.8 copy-done
  293.6 5.8 %all-to-all-start.4 = ((f32[128,80,128]{2,1,0:T(8,128)}), f32[128,80,128]{2,1,0:T(8,128)}, u32[]{:S(2)}, u32[]{:S(2)}) async-start(f32[128,80,128]{2,1,0:T(8,128)} %bitcast.48), calls=%async_computation.4 | async-start | bytes 10485760 | tf_op jit(solution)/shard_map/all_to_all | solution.py:27
  299.4 3.6 join.2.refs_0_
  303.0 61.5 %all-to-all-done.4 = f32[128,80,128]{2,1,0:T(8,128)} async-done(((f32[128,80,128]{2,1,0:T(8,128)}), f32[128,80,128]{2,1,0:T(8,128)}, u32[]{:S(2)}, u32[]{:S(2)}) %all-to-all-start.4) | async-done | bytes 5242912 | tf_op jit(solution)/shard_map/all_to_all | solution.py:27
  364.5 4.9 %join.3 = f32[128,32,4,128]{3,2,1,0:T(4,128)} custom-call(f32[128,20,4,128]{3,2,1,0:T(4,128)} %bitcast.15.src, f32[128,32,4,128]{3,2,1,0:T(4,128)} %join.2.refs_0_), custom_call_target="tpu_custom_call", output_to_operand_aliasing={{}: (1, {})} | custom-call | bytes 10485760 | tf_op jit(solution)/shard_map/join/pallas_call | solution.py:363
  (21 shorter events, 2.8 us)
Async XLA Ops:
  97.0 46.3 %all-to-all-start.2 = ((f32[128,48,128]{2,1,0:T(8,128)}), f32[128,48,128]{2,1,0:T(8,128)S(1)}, u32[]{:S(2)}, u32[]{:S(2)}) async-start(f32[128,48,128]{2,1,0:T(8,128)} %fit.2), calls=%async_computation.2 | async-start | bytes 6291456 | tf_op jit(solution)/shard_map/all_to_all | solution.py:27
  143.3 1.7 copy-start.1
  145.0 70.8 %all-to-all-start.3 = ((f32[128,80,128]{2,1,0:T(8,128)}), f32[128,80,128]{2,1,0:T(8,128)}, u32[]{:S(2)}, u32[]{:S(2)}) async-start(f32[128,80,128]{2,1,0:T(8,128)} %fit.3), calls=%async_computation.3 | async-start | bytes 10485760 | tf_op jit(solution)/shard_map/all_to_all | solution.py:27
  245.2 46.6 %all-to-all-start.5 = ((f32[128,48,128]{2,1,0:T(8,128)}), f32[128,48,128]{2,1,0:T(8,128)S(1)}, u32[]{:S(2)}, u32[]{:S(2)}) async-start(f32[128,48,128]{2,1,0:T(8,128)} %bitcast.51), calls=%async_computation.5 | async-start | bytes 6291456 | tf_op jit(solution)/shard_map/all_to_all | solution.py:27
  291.8 1.8 copy-start
  293.6 70.8 %all-to-all-start.4 = ((f32[128,80,128]{2,1,0:T(8,128)}), f32[128,80,128]{2,1,0:T(8,128)}, u32[]{:S(2)}, u32[]{:S(2)}) async-start(f32[128,80,128]{2,1,0:T(8,128)} %bitcast.48), calls=%async_computation.4 | async-start | bytes 10485760 | tf_op jit(solution)/shard_map/all_to_all | solution.py:27

commit v6 on v5

--- a/solution.py
+++ b/solution.py
@@ -11,7 +11,7 @@
 AXES = ("slab", "wide")
 HI = lax.Precision.HIGHEST
 BLK = 128
-PARTS = (12, 20)
+PARTS = (16, 16)
 SLOTS = 8
 PANEL = 16
 

time: 371 us -> 369 us (level)
  waiting for transfers between devices: 157 us -> 162 us
  Pallas kernels: 139 us -> 135 us
    pallas_call x4, Pallas kernels: 35.8 us -> 30.5 us  [planes(): pl.pallas_call(kernel, out_shape=jax.ShapeDtypeStruct(out_shape, jnp.floa...]
    all_to_all x4, waiting for transfers between devices: 157 us -> 162 us  [exchange(): return lax.all_to_all(blocks, AXES, split_axis=0, concat_axis=0, tiled=True)]
  transfers between devices with their start and end apart: 4 -> 4, of which waited for: 4 -> 4; matrix products, arithmetic and copies ran while one was open for 1% -> 1% of each run, Pallas kernels for 14% -> 13%
where the time goes in v6:
time: 369 us; the launch traced here: 367 us
  waiting for transfers between devices  162 us (44%)
  Pallas kernels  135 us (37%)
  blocking collectives  37.2 us (10%)
  starting transfers between devices  23.5 us (6%)
  other arithmetic  5.61 us (2%)
  local copies, waits for them, and re-layouts  3.84 us (1%)
    all_to_all x4, waiting for transfers between devices, exchange(): return lax.all_to_all(blocks, AXES, split_axis=0, concat_axis=0, tiled=True)  162 us
    all_to_all x2, blocking collectives, exchange(): return lax.all_to_all(blocks, AXES, split_axis=0, concat_axis=0, tiled=True)  37.2 us
    pallas_call x1, Pallas kernels, coefficients(): pl.pallas_call(coeff_kernel, out_shape=[coeff, coeff, sample, sample], sc...  33 us
    pallas_call x4, Pallas kernels, planes(): pl.pallas_call(kernel, out_shape=jax.ShapeDtypeStruct(out_shape, jnp.floa...  30.5 us
    pallas_call x2, Pallas kernels, fit(): pl.pallas_call(fit_kernel, out_shape=jax.ShapeDtypeStruct((vectors, count...  30 us
    all_to_all x4, starting transfers between devices, exchange(): return lax.all_to_all(blocks, AXES, split_axis=0, concat_axis=0, tiled=True)  23.5 us
    pallas_call x2, Pallas kernels, columns(): pl.pallas_call(functools.partial(columns_kernel, start), out_shape=jax.Sh...  22.7 us
    pallas_call x1, Pallas kernels, pick(): pl.pallas_call(pick_kernel, out_shape=jax.ShapeDtypeStruct((npoint, norbi...  9.8 us
  transfers between devices with their start and end apart: 4, of which 4 were waited for; matrix products, arithmetic and copies ran while one was open for 1% of the time, Pallas kernels for 13%

profile of v6, /device:TPU:0, one launch (start us, length us, event | category | flops | bytes accessed | tf_op | source)
XLA Modules:
  0.0 367.2 jit_solution(9062377207688066651)
XLA Ops:
  0.0 0.7 add_select_fusion.5
  0.7 0.7 and_convert_fusion
  1.4 0.6 pad_add_fusion.info
  2.0 9.8 %pick.1 = f32[512,256]{1,0:T(8,128)} custom-call(s32[4,512]{1,0:T(4,128)} %pad_add_fusion.info, f32[256,32,4,128]{3,2,1,0:T(4,128)} %orb.1), custom_call_target="tpu_custom_call" | custom-call | tf_op jit(solution)/shard_map/pick/pallas_call | solution.py:106
  11.8 1.2 reshape.107
  13.0 19.2 %all_to_all.30 = f32[128,4,256]{2,1,0:T(4,128)S(1)} all-to-all(f32[128,4,256]{2,1,0:T(4,128)S(1)} %reshape.107), channel_id=1, replica_groups=mesh['slab'=4,'wide'=32] {'slab','wide'}, dimensions={0} | all-to-all | bytes 1048576 | tf_op jit(solution)/shard_map/all_to_all | solution.py:27
  32.4 18.1 %all_to_all.31 = f32[128,4,256]{2,1,0:T(4,128)S(1)} all-to-all(f32[128,4,256]{2,1,0:T(4,128)S(1)} %broadcast_in_dim.2), channel_id=1, replica_groups=mesh['slab'=4,'wide'=32] {'slab','wide'}, dimensions={0} | all-to-all | bytes 1048576 | tf_op jit(solution)/shard_map/all_to_all | solution.py:27
  50.5 1.0 reshape.108.s_ref
  51.4 33.0 %coefficients.1 = (bf16[128,512]{1,0:T(8,128)(2,1)}, bf16[128,512]{1,0:T(8,128)(2,1)}, bf16[512,256]{1,0:T(8,128)(2,1)}, bf16[512,256]{1,0:T(8,128)(2,1)}) custom-call(f32[512,256]{1,0:T(8,128)} %reshape.108.s_ref), custom_call_target="tpu_custom_call" | custom-call | tf_op jit(solution)/shard_map/coefficients/pallas_call | solution.py:199
  84.4 15.0 %fit.2 = f32[128,64,128]{2,1,0:T(8,128)} custom-call(bf16[512,256]{1,0:T(8,128)(2,1)} %get-tuple-element.12.sh, bf16[512,256]{1,0:T(8,128)(2,1)} %get-tuple-element.13.sl, bf16[128,512]{1,0:T(8,128)(2,1)} %get-tuple-element.14.ch, bf16[128,512]{1,0:T(8,128)(2,1)} %get-tuple-element.15.cl, f32[256,128,128]{2,1,0:T(8,128)} %bitcast.45), custom_call_target="tpu_custom_call" | custom-call | flops 9663676416 | bytes 12582912 | tf_op jit(solution)/shard_map/fit/pallas_call | solution.py:230
  99.4 6.0 %all-to-all-start.2 = ((f32[128,64,128]{2,1,0:T(8,128)}), f32[128,64,128]{2,1,0:T(8,128)}, u32[]{:S(2)}, u32[]{:S(2)}) async-start(f32[128,64,128]{2,1,0:T(8,128)} %fit.2), calls=%async_computation.2 | async-start | bytes 8388608 | tf_op jit(solution)/shard_map/all_to_all | solution.py:27
  105.4 15.1 %fit.3 = f32[128,64,128]{2,1,0:T(8,128)} custom-call(bf16[512,256]{1,0:T(8,128)(2,1)} %get-tuple-element.12.sh, bf16[512,256]{1,0:T(8,128)(2,1)} %get-tuple-element.13.sl, bf16[128,512]{1,0:T(8,128)(2,1)} %get-tuple-element.14.ch, bf16[128,512]{1,0:T(8,128)(2,1)} %get-tuple-element.15.cl, f32[256,128,128]{2,1,0:T(8,128)} %bitcast.46), custom_call_target="tpu_custom_call" | custom-call | flops 9663676416 | bytes 12582912 | tf_op jit(solution)/shard_map/fit/pallas_call | solution.py:230
  120.5 38.1 %all-to-all-done.2 = f32[128,64,128]{2,1,0:T(8,128)} async-done(((f32[128,64,128]{2,1,0:T(8,128)}), f32[128,64,128]{2,1,0:T(8,128)}, u32[]{:S(2)}, u32[]{:S(2)}) %all-to-all-start.2) | async-done | bytes 4194336 | tf_op jit(solution)/shard_map/all_to_all | solution.py:27
  158.6 5.8 %all-to-all-start.3 = ((f32[128,64,128]{2,1,0:T(8,128)}), f32[128,64,128]{2,1,0:T(8,128)}, u32[]{:S(2)}, u32[]{:S(2)}) async-start(f32[128,64,128]{2,1,0:T(8,128)} %fit.3), calls=%async_computation.3 | async-start | bytes 8388608 | tf_op jit(solution)/shard_map/all_to_all | solution.py:27
  165.7 0.8 copy.6.yl
  166.5 0.8 copy.5.yh
  167.2 0.9 reduce-precision_convert_fusion.3
  168.2 0.7 fusion.2
  168.8 0.7 fusion
  169.6 8.2 %planes_in.2 = f32[4,16,128,128]{3,2,1,0:T(8,128)} custom-call(bf16[128,128]{1,0:T(8,128)(2,1)} %get-tuple-element.33.xh, bf16[128,128]{1,0:T(8,128)(2,1)} %get-tuple-element.34.xl, bf16[256,256]{1,0:T(8,128)(2,1)} %copy.5.yh, bf16[256,256]{1,0:T(8,128)(2,1)} %copy.6.yl, f32[4,32,64,128]{3,2,1,0:T(8,128)} %bitcast.11.in_ref), custom_call_target="tpu_custom_call" | custom-call | flops 2415919104 | bytes 8388608 | tf_op jit(solution)/shard_map/planes_in/pallas_call | solution.py:285
  177.7 40.1 %all-to-all-done.3 = f32[128,64,128]{2,1,0:T(8,128)} async-done(((f32[128,64,128]{2,1,0:T(8,128)}), f32[128,64,128]{2,1,0:T(8,128)}, u32[]{:S(2)}, u32[]{:S(2)}) %all-to-all-start.3) | async-done | bytes 4194336 | tf_op jit(solution)/shard_map/all_to_all | solution.py:27
  217.8 8.2 %planes_in.3 = f32[4,16,128,128]{3,2,1,0:T(8,128)} custom-call(bf16[128,128]{1,0:T(8,128)(2,1)} %get-tuple-element.33.xh, bf16[128,128]{1,0:T(8,128)(2,1)} %get-tuple-element.34.xl, bf16[256,256]{1,0:T(8,128)(2,1)} %copy.5.yh, bf16[256,256]{1,0:T(8,128)(2,1)} %copy.6.yl, f32[4,32,64,128]{3,2,1,0:T(8,128)} %bitcast.13.in_ref), custom_call_target="tpu_custom_call" | custom-call | flops 2415919104 | bytes 8388608 | tf_op jit(solution)/shard_map/planes_in/pallas_call | solution.py:285
  225.9 11.4 %columns.3 = f32[64,128,128]{2,1,0:T(8,128)} custom-call(bf16[2,128,128]{2,1,0:T(8,128)(2,1)} %get-tuple-element.26.zh, bf16[2,128,128]{2,1,0:T(8,128)(2,1)} %get-tuple-element.25.zl, f32[64,128,128]{2,1,0:T(8,128)} %bitcast.41, f32[64,128,128]{2,1,0:T(8,128)} %bitcast.43), custom_call_target="tpu_custom_call" | custom-call | flops 2415919104 | bytes 12582912 | tf_op jit(solution)/shard_map/columns/pallas_call | solution.py:332
  237.3 7.1 %planes_out.3 = f32[4,32,64,128]{3,2,1,0:T(8,128)} custom-call(bf16[128,128]{1,0:T(8,128)(2,1)} %get-tuple-element.33.xh, bf16[128,128]{1,0:T(8,128)(2,1)} %get-tuple-element.34.xl, bf16[256,256]{1,0:T(8,128)(2,1)} %get-tuple-element.24.yh, bf16[256,256]{1,0:T(8,128)(2,1)} %get-tuple-element.23.yl, f32[4,16,128,128]{3,2,1,0:T(8,128)} %bitcast.48), custom_call_target="tpu_custom_call" | custom-call | flops 2415919104 | bytes 8388608 | tf_op jit(solution)/shard_map/planes_out/pallas_call | solution.py:285
  244.4 5.8 %all-to-all-start.5 = ((f32[128,64,128]{2,1,0:T(8,128)}), f32[128,64,128]{2,1,0:T(8,128)}, u32[]{:S(2)}, u32[]{:S(2)}) async-start(f32[128,64,128]{2,1,0:T(8,128)} %bitcast.49), calls=%async_computation.5 | async-start | bytes 8388608 | tf_op jit(solution)/shard_map/all_to_all | solution.py:27
  250.3 11.4 %columns.2 = f32[64,128,128]{2,1,0:T(8,128)} custom-call(bf16[2,128,128]{2,1,0:T(8,128)(2,1)} %get-tuple-element.26.zh, bf16[2,128,128]{2,1,0:T(8,128)(2,1)} %get-tuple-element.25.zl, f32[64,128,128]{2,1,0:T(8,128)} %bitcast.42, f32[64,128,128]{2,1,0:T(8,128)} %bitcast.44), custom_call_target="tpu_custom_call" | custom-call | flops 2415919104 | bytes 12582912 | tf_op jit(solution)/shard_map/columns/pallas_call | solution.py:332
  261.6 7.1 %planes_out.2 = f32[4,32,64,128]{3,2,1,0:T(8,128)} custom-call(bf16[128,128]{1,0:T(8,128)(2,1)} %get-tuple-element.33.xh, bf16[128,128]{1,0:T(8,128)(2,1)} %get-tuple-element.34.xl, bf16[256,256]{1,0:T(8,128)(2,1)} %get-tuple-element.24.yh, bf16[256,256]{1,0:T(8,128)(2,1)} %get-tuple-element.23.yl, f32[4,16,128,128]{3,2,1,0:T(8,128)} %bitcast.47), custom_call_target="tpu_custom_call" | custom-call | flops 2415919104 | bytes 8388608 | tf_op jit(solution)/shard_map/planes_out/pallas_call | solution.py:285
  268.7 34.9 %all-to-all-done.5 = f32[128,64,128]{2,1,0:T(8,128)} async-done(((f32[128,64,128]{2,1,0:T(8,128)}), f32[128,64,128]{2,1,0:T(8,128)}, u32[]{:S(2)}, u32[]{:S(2)}) %all-to-all-start.5) | async-done | bytes 4194336 | tf_op jit(solution)/shard_map/all_to_all | solution.py:27
  303.6 5.8 %all-to-all-start.4 = ((f32[128,64,128]{2,1,0:T(8,128)}), f32[128,64,128]{2,1,0:T(8,128)}, u32[]{:S(2)}, u32[]{:S(2)}) async-start(f32[128,64,128]{2,1,0:T(8,128)} %bitcast.50), calls=%async_computation.4 | async-start | bytes 8388608 | tf_op jit(solution)/shard_map/all_to_all | solution.py:27
  309.4 4.2 %join.2.refs_0_ = f32[128,32,4,128]{3,2,1,0:T(4,128)} custom-call(f32[128,16,4,128]{3,2,1,0:T(4,128)} %bitcast.20.src), custom_call_target="tpu_custom_call" | custom-call | bytes 8388608 | tf_op jit(solution)/shard_map/join/pallas_call | solution.py:363
  313.7 49.1 %all-to-all-done.4 = f32[128,64,128]{2,1,0:T(8,128)} async-done(((f32[128,64,128]{2,1,0:T(8,128)}), f32[128,64,128]{2,1,0:T(8,128)}, u32[]{:S(2)}, u32[]{:S(2)}) %all-to-all-start.4) | async-done | bytes 4194336 | tf_op jit(solution)/shard_map/all_to_all | solution.py:27
  362.8 4.2 %join.3 = f32[128,32,4,128]{3,2,1,0:T(4,128)} custom-call(f32[128,16,4,128]{3,2,1,0:T(4,128)} %bitcast.17.src, f32[128,32,4,128]{3,2,1,0:T(4,128)} %join.2.refs_0_), custom_call_target="tpu_custom_call", output_to_operand_aliasing={{}: (1, {})} | custom-call | bytes 8388608 | tf_op jit(solution)/shard_map/join/pallas_call | solution.py:363
  (13 shorter events, 1.5 us)
Async XLA Ops:
  99.4 59.2 %all-to-all-start.2 = ((f32[128,64,128]{2,1,0:T(8,128)}), f32[128,64,128]{2,1,0:T(8,128)}, u32[]{:S(2)}, u32[]{:S(2)}) async-start(f32[128,64,128]{2,1,0:T(8,128)} %fit.2), calls=%async_computation.2 | async-start | bytes 8388608 | tf_op jit(solution)/shard_map/all_to_all | solution.py:27
  158.6 59.2 %all-to-all-start.3 = ((f32[128,64,128]{2,1,0:T(8,128)}), f32[128,64,128]{2,1,0:T(8,128)}, u32[]{:S(2)}, u32[]{:S(2)}) async-start(f32[128,64,128]{2,1,0:T(8,128)} %fit.3), calls=%async_computation.3 | async-start | bytes 8388608 | tf_op jit(solution)/shard_map/all_to_all | solution.py:27
  244.4 59.2 %all-to-all-start.5 = ((f32[128,64,128]{2,1,0:T(8,128)}), f32[128,64,128]{2,1,0:T(8,128)}, u32[]{:S(2)}, u32[]{:S(2)}) async-start(f32[128,64,128]{2,1,0:T(8,128)} %bitcast.49), calls=%async_computation.5 | async-start | bytes 8388608 | tf_op jit(solution)/shard_map/all_to_all | solution.py:27
  303.6 59.2 %all-to-all-start.4 = ((f32[128,64,128]{2,1,0:T(8,128)}), f32[128,64,128]{2,1,0:T(8,128)}, u32[]{:S(2)}, u32[]{:S(2)}) async-start(f32[128,64,128]{2,1,0:T(8,128)} %bitcast.50), calls=%async_computation.4 | async-start | bytes 8388608 | tf_op jit(solution)/shard_map/all_to_all | solution.py:27
